TPU v7x, 32 devices: a whole 2x2x4 slice. The times are simulated.
32 devices in a mesh: seq: 8 (over y, x, core), dp: 4 (over z).
Axes of the slice: x: 2, y: 2, z: 4, core: 2. Of those that a mesh axis runs over, the one named last changes fastest.
Arguments:
- tokens: bfloat16 [4, 4096, 1024], P('dp', 'seq'), may hold values from -6 to 6
- item_starts: int32 [4, 8], P('dp', 'seq'), may hold values from 0 to 1, as said below
- attn_gain: float32 [1024], replicated, may hold values from 0.5 to 1.5
- query_weight: bfloat16 [1024, 1024], replicated, may hold values from -0.1875 to 0.1875
- key_weight: bfloat16 [1024, 1024], replicated, may hold values from -0.1875 to 0.1875
- value_weight: bfloat16 [1024, 1024], replicated, may hold values from -0.1875 to 0.1875
- output_weight: bfloat16 [1024, 1024], replicated, may hold values from -1.5 to 1.5
- state_queries: bfloat16 [512, 1024], replicated, may hold values from -6 to 6
- state_weight: bfloat16 [1024, 2048], replicated, may hold values from -1.5 to 1.5
- gate_bias: float32 [1024], replicated, may hold values from -2 to 6
- initial_state: float32 [512, 1024], replicated, may hold values from -6 to 6
- mlp_gain: float32 [1024], replicated, may hold values from 0.5 to 1.5
- up_weight: bfloat16 [1024, 4096], replicated, may hold values from -0.1875 to 0.1875
- down_weight: bfloat16 [4096, 1024], replicated, may hold values from -0.09375 to 0.09375
- out_cotangent: bfloat16 [4, 4096, 1024], P('dp', 'seq'), may hold values from -6 to 6
- state_cotangent: float32 [4, 8, 512, 1024], P('dp', 'seq'), may hold values from -6 to 6
Outputs:
- mixed: bfloat16 [4, 4096, 1024], P('dp', 'seq')
- states: float32 [4, 8, 512, 1024], P('dp', 'seq')
- tokens_grad: float32 [4, 4096, 1024], P('dp', 'seq')
- attn_gain_grad: float32 [1024], P('seq')
- query_grad: float32 [1024, 1024], P('seq')
- key_grad: float32 [1024, 1024], P('seq')
- value_grad: float32 [1024, 1024], P('seq')
- output_grad: float32 [1024, 1024], P('seq')
- state_queries_grad: float32 [512, 1024], P('seq')
- state_weight_grad: float32 [1024, 2048], P('seq')
- gate_bias_grad: float32 [1024], P('seq')
- initial_state_grad: float32 [512, 1024], P('seq')
- mlp_gain_grad: float32 [1024], P('seq')
- up_grad: float32 [1024, 4096], P('seq')
- down_grad: float32 [4096, 1024], P('seq')
Inputs may be any that keep to these rules, and one draw needn't show every extreme that they name: item_starts is 1 exactly at the first block of each item. Block 0 of every group starts an item; each aligned run of 8 blocks holds one item of 8 blocks or two of 4 blocks; some item has 8 blocks.
All inputs are finite; a program needn't handle non-finite values.
Results may differ from a plain program's by a relative error of at most 0.023.
Values may be sent and summed in bfloat16 or wider, within the bound.
No kernel may reach another device: no remote copies, remote signals or barrier semaphores. Data moves between devices by JAX's collectives and lax.ppermute only.
A program may use at most 512 MiB of HBM per device.

v0:
```python
import functools
import math

import jax
import jax.numpy as jnp
from jax import lax
from jax.experimental import pallas as pl
from jax.experimental.pallas import tpu as pltpu
from jax.sharding import PartitionSpec as P

D = 1024
HEADS = 8
HEAD_DIM = 128
FF = 4096
W = 512
NS = 512
HALF = NS // 2
QUARTER = NS // 8

EPSILON = 1e-06
NEGATIVE = -1e30
GELU_SCALE = 0.7978845608028654
GELU_CUBIC = 0.044715
SCALE = 1.0 / math.sqrt(HEAD_DIM)
SCALE_LOG2 = SCALE * math.log2(math.e)

BF = jnp.bfloat16
F32 = jnp.float32
MIB = 1 << 20
LONG = 1e11


def swapped(value, axis, distance):
    count = lax.axis_size(axis)
    return lax.ppermute(value, axis, [(place, place ^ distance) for place in range(count)])


def shifted(value, axis, steps):
    count = lax.axis_size(axis)
    first, last = (max(0, -steps), min(count, count - steps))
    return lax.ppermute(value, axis, [(source, source + steps) for source in range(first, last)])


def add_low(*terms):
    total = terms[0].astype(F32)
    for term in terms[1:]:
        total = total + term.astype(F32)
    return total.astype(BF)


def pick(value, index, axis):
    return lax.dynamic_index_in_dim(value, index, axis, False)


def product(left, right):
    return jnp.dot(left, right, preferred_element_type=F32)


def product_tn(left, right):
    return lax.dot_general(left, right, (((0,), (0,)), ((), ())), preferred_element_type=F32)


def product_nt(left, right):
    return lax.dot_general(left, right, (((1,), (1,)), ((), ())), preferred_element_type=F32)


def rms_scale(field):
    return lax.rsqrt(jnp.mean(field * field, axis=-1, keepdims=True) + EPSILON)


def shape(dims, dtype):
    return jax.ShapeDtypeStruct(dims, dtype)


def whole(dims):
    return pl.BlockSpec(dims, lambda *_: (0,) * len(dims))


def fixed(dims):
    return pl.BlockSpec(dims, lambda *_: (0,) * len(dims), pipeline_mode=pl.Buffered(1))


class Clock:
    def __init__(self, flags):
        self.flags = flags

    def after(self, *values):
        self.flags = lax.optimization_barrier((self.flags, values))[0]

    def at(self, value):
        return lax.optimization_barrier((value, self.flags))[0]

    def run(self, kernel, outs, args, grid, in_specs, out_specs, scratch=(), flops=0, limit=20, stream=False):
        nbytes = sum(math.prod(a.shape) * a.dtype.itemsize for a in args) + sum(
            math.prod(o.shape) * o.dtype.itemsize for o in outs
        )
        args = [
            pltpu.with_memory_space_constraint(arg, pltpu.HBM)
            if stream and spec.block_shape != arg.shape
            else arg
            for arg, spec in zip(args, in_specs)
        ]
        results = pl.pallas_call(
            kernel,
            out_shape=outs,
            grid_spec=pltpu.PrefetchScalarGridSpec(
                num_scalar_prefetch=1,
                grid=grid,
                in_specs=in_specs,
                out_specs=out_specs,
                scratch_shapes=list(scratch),
            ),
            compiler_params=pltpu.CompilerParams(
                dimension_semantics=("arbitrary",) * len(grid), vmem_limit_bytes=limit * MIB
            ),
            cost_estimate=pl.CostEstimate(
                flops=int(flops), bytes_accessed=int(nbytes), transcendentals=0
            ),
        )(self.flags, *args)
        self.after(results[0])
        return results


START, CORE, CHIP = 0, 1, 2


def front_kernel(flags, tokens, gain, wq, wk, wv, normed, queries, pair):
    @pl.when(pl.program_id(0) == 0)
    def _():
        inputs = tokens[...].astype(F32)
        normed[...] = (inputs * rms_scale(inputs) * gain[...]).astype(BF)

    rows = normed[...]
    queries[...] = product(rows, wq[...]).astype(BF)
    pair[0] = product(rows, wk[...]).astype(BF)
    pair[1] = product(rows, wv[...]).astype(BF)


def front(clock, tokens, gain, wq, wk, wv):
    step = 256
    column = pl.BlockSpec((D, step), lambda j, *_: (0, j))
    return clock.run(
        front_kernel,
        (shape((W, D), BF), shape((W, D), BF), shape((2, W, D), BF)),
        (tokens, gain, wq, wk, wv),
        (D // step,),
        [whole((W, D)), whole((1, D)), column, column, column],
        (
            whole((W, D)),
            pl.BlockSpec((W, step), lambda j, *_: (0, j)),
            pl.BlockSpec((2, W, step), lambda j, *_: (0, 0, j)),
        ),
        flops=6 * W * D * D,
        stream=True,
    )


def left_kernel(flags, tokens, gain, wk, wv, pair, normed):
    @pl.when(pl.program_id(0) == 0)
    def _():
        inputs = tokens[...].astype(F32)
        normed[...] = (inputs * rms_scale(inputs) * gain[...]).astype(BF)

    rows = normed[...]
    pair[0] = product(rows, wk[...]).astype(BF)
    pair[1] = product(rows, wv[...]).astype(BF)


def left_pair(clock, tokens, gain, wk, wv):
    step = 256
    column = pl.BlockSpec((D, step), lambda j, *_: (0, j))
    return clock.run(
        left_kernel,
        (shape((2, W, D), BF),),
        (tokens, gain, wk, wv),
        (D // step,),
        [whole((W, D)), whole((1, D)), column, column],
        (pl.BlockSpec((2, W, step), lambda j, *_: (0, 0, j)),),
        [pltpu.VMEM((W, D), BF)],
        flops=LONG,
    )[0]


def summary_probs_of(keys, asks):
    raw = product_nt(keys, asks) * SCALE_LOG2
    expos = jnp.exp2(raw - jnp.max(raw, axis=0, keepdims=True))
    return expos, jnp.sum(expos, axis=0, keepdims=True)


def gates_kernel(
    flags, asks, pair, wu, wg, bias, initial, summary, forget, update, give, own, work
):
    step = pl.program_id(0)

    @pl.when(step < 4)
    def _():
        for head in range(2):
            at = slice(head * HEAD_DIM, (head + 1) * HEAD_DIM)
            expos, total = summary_probs_of(pair[0, :, at], asks[:, at])
            held = product_tn(pair[1, :, at], expos.astype(BF)) / total
            place = pl.multiple_of(step * 256 + head * HEAD_DIM, HEAD_DIM)
            summary[:, pl.ds(place, HEAD_DIM)] = held.T.astype(BF)

    @pl.when(step >= 4)
    def _():
        start = flags[START].astype(F32)
        rows = summary[...]
        fresh = product(rows, wu[...])
        gate = jax.nn.sigmoid(product(rows, wg[...]) + bias[...])
        update[...] = fresh
        forget[...] = gate
        work[0] = (1.0 - start) * gate
        work[1] = start * gate * initial[...] + (1.0 - gate) * fresh
        mine = pl.multiple_of(flags[CORE] * HALF, HALF)
        others = pl.multiple_of((1 - flags[CORE]) * HALF, HALF)
        for part in range(2):
            own[part] = work[part, pl.ds(mine, HALF)].astype(BF)
            give[part] = work[part, pl.ds(others, HALF)].astype(BF)


def gates(clock, asks, pair, state_weight, bias, initial):
    step = 256
    early = lambda i, *_: (0, jnp.minimum(i, 3))
    late = lambda i, *_: (0, jnp.maximum(i - 4, 0))
    late3 = lambda i, *_: (0, 0, jnp.maximum(i - 4, 0))
    return clock.run(
        gates_kernel,
        (
            shape((NS, D), BF),
            shape((NS, D), F32),
            shape((NS, D), F32),
            shape((2, HALF, D), BF),
            shape((2, HALF, D), BF),
        ),
        (asks, pair, state_weight, state_weight, bias, initial),
        (8,),
        [
            pl.BlockSpec((NS, step), early),
            pl.BlockSpec((2, W, step), lambda i, *_: (0, 0, jnp.minimum(i, 3))),
            pl.BlockSpec((D, step), late),
            pl.BlockSpec((D, step), lambda i, *_: (0, jnp.maximum(i - 4, 0) + D // step)),
            pl.BlockSpec((1, step), late),
            pl.BlockSpec((NS, step), late),
        ],
        (
            whole((NS, D)),
            pl.BlockSpec((NS, step), late),
            pl.BlockSpec((NS, step), late),
            pl.BlockSpec((2, HALF, step), late3),
            pl.BlockSpec((2, HALF, step), late3),
        ),
        [pltpu.VMEM((2, NS, step), F32)],
        flops=4 * NS * W * D + 4 * NS * D * D,
    )


def rows_of(chip):
    return pl.ds(pl.multiple_of(chip * QUARTER, QUARTER), QUARTER)


def compose_kernel(flags, own, recv, keep, to1, to2, to3, work):
    odd_core = flags[CORE] == 1
    pick2 = lambda part: (own[part].astype(F32), recv[part].astype(F32))
    (own_scale, recv_scale), (own_base, recv_base) = pick2(0), pick2(1)
    later_scale = jnp.where(odd_core, own_scale, recv_scale)
    earlier_base = jnp.where(odd_core, recv_base, own_base)
    later_base = jnp.where(odd_core, own_base, recv_base)
    work[0] = own_scale * recv_scale
    work[1] = later_scale * earlier_base + later_base
    for far, out in enumerate((keep, to1, to2, to3)):
        out[...] = work[:, rows_of(flags[CHIP] ^ far)].astype(BF)


def prefix_kernel(flags, keep, from1, from2, from3, mine, to1, to2, to3, got, enter):
    for far, came in enumerate((keep, from1, from2, from3)):
        got[flags[CHIP] ^ far] = came[...].astype(F32)
    state = got[0, 1]
    enter[0] = jnp.zeros_like(state)
    enter[1] = state
    for chip in (1, 2):
        state = got[chip, 0] * state + got[chip, 1]
        enter[chip + 1] = state
    for far, out in enumerate((mine, to1, to2, to3)):
        out[...] = enter[flags[CHIP] ^ far].astype(BF)


def previous_kernel(flags, mine, from1, from2, from3, own, recv, keep, give, before):
    for far, came in enumerate((mine, from1, from2, from3)):
        before[rows_of(flags[CHIP] ^ far)] = came[...].astype(F32)
    odd_core = flags[CORE] == 1
    scale = jnp.where(odd_core, recv[0].astype(F32), own[0].astype(F32))
    base = jnp.where(odd_core, recv[1].astype(F32), own[1].astype(F32))
    entry = before[...]
    between = scale * entry + base
    keep[...] = jnp.where(odd_core, between, entry).astype(BF)
    give[...] = jnp.where(odd_core, entry, between).astype(BF)


def compose_back_kernel(flags, own, recv, own_pair, recv_pair, keep, to1, to2, to3, work):
    odd_core = flags[CORE] == 1
    scale = jnp.where(odd_core, recv_pair[0].astype(F32), own_pair[0].astype(F32))
    mine, other = own[...].astype(F32), recv[...].astype(F32)
    work[...] = scale * jnp.where(odd_core, mine, other) + jnp.where(odd_core, other, mine)
    for far, out in enumerate((keep, to1, to2, to3)):
        out[...] = work[rows_of(flags[CHIP] ^ far)].astype(BF)


def suffix_kernel(
    flags, keep, from1, from2, from3, kept0, kept1, kept2, kept3, mine, to1, to2, to3, got, enter
):
    pairs = ((keep, kept0), (from1, kept1), (from2, kept2), (from3, kept3))
    for far, (came, kept) in enumerate(pairs):
        got[flags[CHIP] ^ far, 0] = kept[0].astype(F32)
        got[flags[CHIP] ^ far, 1] = came[...].astype(F32)
    state = got[3, 1]
    enter[3] = jnp.zeros_like(state)
    enter[2] = state
    for chip in (2, 1):
        state = got[chip, 0] * state + got[chip, 1]
        enter[chip - 1] = state
    for far, out in enumerate((mine, to1, to2, to3)):
        out[...] = enter[flags[CHIP] ^ far].astype(BF)


def following_kernel(
    flags, mine, from1, from2, from3, own, recv, own_pair, recv_pair, keep, give, after
):
    for far, came in enumerate((mine, from1, from2, from3)):
        after[rows_of(flags[CHIP] ^ far)] = came[...].astype(F32)
    odd_core = flags[CORE] == 1
    scale = jnp.where(odd_core, own_pair[0].astype(F32), recv_pair[0].astype(F32))
    base = jnp.where(odd_core, own[...].astype(F32), recv[...].astype(F32))
    entry = after[...]
    between = scale * entry + base
    keep[...] = jnp.where(odd_core, entry, between).astype(BF)
    give[...] = jnp.where(odd_core, between, entry).astype(BF)


def small(clock, kernel, outs, args, scratch):
    return clock.run(
        kernel,
        tuple(shape(dims, BF) for dims in outs),
        args,
        (1,),
        [whole(a.shape) for a in args],
        tuple(whole(dims) for dims in outs),
        [pltpu.VMEM(dims, F32) for dims in scratch],
        limit=10,
    )


def to_chips(values):
    return (values[0],) + tuple(
        swapped(value, "seq", 2 * far) for far, value in zip((1, 2, 3), values[1:])
    )


PAIR_WORK = [(4, 2, QUARTER, D), (4, QUARTER, D)]


def compose(clock, own, recv):
    return to_chips(small(clock, compose_kernel, [(2, QUARTER, D)] * 4, (own, recv), [(2, HALF, D)]))


def prefix(clock, got):
    return to_chips(small(clock, prefix_kernel, [(QUARTER, D)] * 4, got, PAIR_WORK))


def previous(clock, back, own, recv):
    mine, other = small(
        clock, previous_kernel, [(HALF, D)] * 2, back + (own, recv), [(HALF, D)]
    )
    return mine, swapped(other, "seq", 1)


def compose_back(clock, *args):
    return to_chips(small(clock, compose_back_kernel, [(QUARTER, D)] * 4, args, [(HALF, D)]))


def suffix(clock, got, kept):
    return to_chips(small(clock, suffix_kernel, [(QUARTER, D)] * 4, got + kept, PAIR_WORK))


def following(clock, back, *args):
    mine, other = small(clock, following_kernel, [(HALF, D)] * 2, back + args, [(HALF, D)])
    return mine, swapped(other, "seq", 1)


def state_kernel(
    flags, mine, other, initial, forget, update, wk, wv, state_in, state_low, state_out, pair
):
    @pl.when(pl.program_id(0) == 0)
    def _():
        start = flags[START].astype(F32)
        for core, came in ((flags[CORE], mine), (1 - flags[CORE], other)):
            rows = pl.ds(pl.multiple_of(core * HALF, HALF), HALF)
            entry = (1.0 - start) * came[...].astype(F32) + start * initial[rows, :]
            gate = forget[rows, :]
            state_in[rows, :] = entry
            state_low[rows, :] = entry.astype(BF)
            state_out[rows, :] = gate * entry + (1.0 - gate) * update[rows, :]

    rows = state_low[...]
    pair[0] = product(rows, wk[...]).astype(BF)
    pair[1] = product(rows, wv[...]).astype(BF)


def state_pair(clock, mine, other, initial, forget, update, wk, wv):
    step = 256
    column = pl.BlockSpec((D, step), lambda j, *_: (0, j))
    return clock.run(
        state_kernel,
        (shape((NS, D), F32), shape((NS, D), BF), shape((NS, D), F32), shape((2, NS, D), BF)),
        (mine, other, initial, forget, update, wk, wv),
        (D // step,),
        [whole((HALF, D))] * 2 + [whole((NS, D))] * 3 + [column, column],
        (
            whole((NS, D)),
            whole((NS, D)),
            whole((NS, D)),
            pl.BlockSpec((2, NS, step), lambda j, *_: (0, 0, j)),
        ),
        flops=4 * NS * D * D,
    )


def masked_scores(flags, queries, left, own, state):
    seen = []
    left_bias = jnp.where(flags[START] == 0, 0.0, NEGATIVE).astype(F32)
    seen.append(product_nt(left[0], queries) * SCALE_LOG2 + left_bias)
    rows = lax.broadcasted_iota(jnp.int32, (W, W), 0)
    cols = lax.broadcasted_iota(jnp.int32, (W, W), 1)
    seen.append(jnp.where(rows <= cols, product_nt(own[0], queries) * SCALE_LOG2, NEGATIVE))
    seen.append(product_nt(state[0], queries) * SCALE_LOG2)
    return seen


PER_STEP = 2


def each_head(*refs):
    for head in range(PER_STEP):
        at = pl.ds(head * HEAD_DIM, HEAD_DIM)
        yield head, [ref.at[..., at] for ref in refs]


def attend_kernel(flags, *refs):
    lse = refs[-1]
    for head, (queries, left, own, state, attended) in each_head(*refs[:-1]):
        seen = masked_scores(flags, queries[...], left, own, state)
        peak = functools.reduce(
            jnp.maximum, [jnp.max(part, axis=0, keepdims=True) for part in seen]
        )
        held = 0.0
        total = 0.0
        for part, pair in zip(seen, (left, own, state)):
            expos = jnp.exp2(part - peak)
            total = total + jnp.sum(expos, axis=0, keepdims=True)
            held = held + product_tn(pair[1], expos.astype(BF))
        attended[...] = (held / total).T.astype(BF)
        lse[head] = peak + jnp.log2(total)


HEADS_WIDE = PER_STEP * HEAD_DIM


def attend(clock, queries, left, own, state):
    head = pl.BlockSpec((W, HEADS_WIDE), lambda h, *_: (0, h))
    pair = pl.BlockSpec((2, W, HEADS_WIDE), lambda h, *_: (0, 0, h))
    return clock.run(
        attend_kernel,
        (shape((W, D), BF), shape((HEADS, 1, W), F32)),
        (queries, left, own, state),
        (HEADS // PER_STEP,),
        [head, pair, pair, pair],
        (head, pl.BlockSpec((PER_STEP, 1, W), lambda h, *_: (h, 0, 0))),
        flops=4 * W * (2 * W + NS) * D,
        stream=True,
        limit=26,
    )


def attend_back_kernel(flags, queries, left, own, state, grad, lse, *outs):
    for head, (asks, left_h, own_h, state_h, grad_h, queries_grad, *grads) in each_head(
        queries, left, own, state, grad, *outs
    ):
        asks, out_grad = asks[...], grad_h[...]
        pairs = (left_h, own_h, state_h)
        seen = masked_scores(flags, asks, *pairs)
        probs = [jnp.exp2(part - lse[head]) for part in seen]
        prob_grads = [product_nt(pair[1], out_grad) for pair in pairs]
        rowdot = sum(
            jnp.sum(prob * prob_grad, axis=0, keepdims=True)
            for prob, prob_grad in zip(probs, prob_grads)
        )
        total = 0.0
        for prob, prob_grad, pair, out in zip(probs, prob_grads, pairs, grads):
            score_grad = (prob * (prob_grad - rowdot)).astype(BF)
            out[0] = (product(score_grad, asks) * SCALE).astype(out.dtype)
            out[1] = product(prob.astype(BF), out_grad).astype(out.dtype)
            total = total + product_tn(pair[0], score_grad)
        queries_grad[...] = (total * SCALE).T.astype(BF)


def attend_back(clock, queries, left, own, state, grad, lse):
    head = pl.BlockSpec((W, HEADS_WIDE), lambda h, *_: (0, h))
    pair = pl.BlockSpec((2, W, HEADS_WIDE), lambda h, *_: (0, 0, h))
    return clock.run(
        attend_back_kernel,
        (shape((W, D), BF), shape((2, W, D), BF), shape((2, W, D), F32), shape((2, NS, D), BF)),
        (queries, left, own, state, grad, lse),
        (HEADS // PER_STEP,),
        [head, pair, pair, pair, head, pl.BlockSpec((PER_STEP, 1, W), lambda h, *_: (h, 0, 0))],
        (head, pair, pair, pair),
        flops=10 * W * (2 * W + NS) * D,
        stream=True,
        limit=36,
    )


def gelu_parts(upper):
    square = upper * upper
    inner = GELU_SCALE * (upper + GELU_CUBIC * square * upper)
    bent = jnp.tanh(inner)
    value = 0.5 * upper * (1.0 + bent)
    slope = 0.5 * (1.0 + bent) + 0.5 * upper * (1.0 - bent * bent) * GELU_SCALE * (
        1.0 + 3.0 * GELU_CUBIC * square
    )
    return value, slope


def mlp_step(normed_mlp, come, up1, up2, down, up, activated, upper_grad, total, grad):
    half = up1.shape[1]
    up[:, :half] = up1[...]
    up[:, half:] = up2[...]
    rows = down[...].reshape(2 * half, D)
    value, slope = gelu_parts(product(normed_mlp[...], up[...]))
    value = value.astype(BF)
    activated[...] = value
    total[...] += product(value, rows)
    back = (come[...].astype(F32) * slope).astype(BF)
    upper_grad[...] = back
    grad[...] += product_nt(back, up[...])


def come_kernel(flags, cotangent, down1, down2, come1, come2):
    for down, come in ((down1, come1), (down2, come2)):
        rows = down[...].reshape(come.shape[1], D)
        come[...] = product_nt(cotangent[...], rows).astype(BF)


def come_back(clock, cotangent, down):
    return clock.run(
        come_kernel,
        (shape((W, FF // 2), BF),) * 2,
        (cotangent, down, down),
        (PAIRS,),
        [fixed((W, D)), mlp_specs(0)[2], mlp_specs(1)[2]],
        (mlp_halves(),) * 2,
        flops=2 * W * D * FF,
    )


def mlp_first_kernel(
    flags,
    attended,
    tokens,
    out_weight,
    gain,
    come,
    up1,
    up2,
    down,
    activated,
    upper_grad,
    normed_mlp,
    hidden,
    total,
    grad,
    up,
):
    @pl.when(pl.program_id(0) == 0)
    def _():
        field = tokens[...].astype(F32) + product(attended[...], out_weight[...])
        hidden[...] = field
        normed_mlp[...] = (field * rms_scale(field) * gain[...]).astype(BF)
        total[...] = field
        grad[...] = jnp.zeros_like(field)

    mlp_step(normed_mlp, come, up1, up2, down, up, activated, upper_grad, total, grad)


def mlp_second_kernel(
    flags,
    normed_mlp,
    hidden,
    total_in,
    grad_in,
    out_weight,
    gain,
    cotangent,
    come,
    up1,
    up2,
    down,
    activated,
    upper_grad,
    mixed,
    hidden_grad,
    attended_grad,
    heads_grad,
    gain_grad,
    total,
    grad,
    up,
):
    step = pl.program_id(0)

    @pl.when(step == 0)
    def _():
        total[...] = total_in[...]
        grad[...] = grad_in[...]

    mlp_step(normed_mlp, come, up1, up2, down, up, activated, upper_grad, total, grad)

    @pl.when(step == pl.num_programs(0) - 1)
    def _():
        mixed[...] = total[...].astype(BF)
        field = hidden[...]
        scaled = rms_scale(field)
        gain_grad[...] = jnp.sum(grad[...] * field * scaled, axis=0, keepdims=True)
        weighted = grad[...] * gain[...]
        field_grad = (
            cotangent[...].astype(F32)
            + scaled * weighted
            - field
            * (scaled * scaled * scaled * jnp.mean(weighted * field, axis=-1, keepdims=True))
        )
        hidden_grad[...] = field_grad
        low = field_grad.astype(BF)
        attended_grad[...] = low
        heads_grad[...] = product_nt(low, out_weight[...]).astype(BF)


PIECE = 256
PAIRS = FF // (4 * PIECE)


def mlp_specs(part):
    return [
        pl.BlockSpec((D, PIECE), lambda j, *_: (0, 4 * j + part)),
        pl.BlockSpec((D, PIECE), lambda j, *_: (0, 4 * j + 2 + part)),
        pl.BlockSpec((2, PIECE, D), lambda j, *_: (j, part, 0)),
    ]


def mlp_halves():
    return pl.BlockSpec((W, 2 * PIECE), lambda j, *_: (0, j))


def mlp_first(clock, attended, tokens, out_weight, gain, come, up, down):
    rows = whole((W, D))
    return clock.run(
        mlp_first_kernel,
        (
            shape((W, FF // 2), BF),
            shape((W, FF // 2), BF),
            shape((W, D), BF),
            shape((W, D), F32),
            shape((W, D), F32),
            shape((W, D), F32),
        ),
        (attended, tokens, out_weight, gain, come, up, up, down),
        (PAIRS,),
        [fixed((W, D)), fixed((W, D)), fixed((D, D)), fixed((1, D)), mlp_halves()] + mlp_specs(0),
        (mlp_halves(), mlp_halves(), rows, rows, rows, rows),
        [pltpu.VMEM((D, 2 * PIECE), BF)],
        flops=3 * W * D * FF + 2 * W * D * D,
        limit=36,
    )


def mlp_second(
    clock, normed_mlp, hidden, total, grad, out_weight, gain, cotangent, come, up, down
):
    rows = whole((W, D))
    return clock.run(
        mlp_second_kernel,
        (
            shape((W, FF // 2), BF),
            shape((W, FF // 2), BF),
            shape((W, D), BF),
            shape((W, D), F32),
            shape((W, D), BF),
            shape((W, D), BF),
            shape((1, D), F32),
        ),
        (normed_mlp, hidden, total, grad, out_weight, gain, cotangent, come, up, up, down),
        (PAIRS,),
        [fixed((W, D))] * 4
        + [fixed((D, D)), fixed((1, D)), fixed((W, D)), mlp_halves()]
        + mlp_specs(1),
        (mlp_halves(), mlp_halves(), rows, rows, rows, rows, whole((1, D))),
        [pltpu.VMEM((W, D), F32), pltpu.VMEM((W, D), F32), pltpu.VMEM((D, 2 * PIECE), BF)],
        flops=3 * W * D * FF + 2 * W * D * D,
        limit=36,
    )


def direct_kernel(flags, state_grad, wk, wv, forget, cotangent, direct, own, give, work):
    grad = product_nt(state_grad[0], wk[...]) + product_nt(state_grad[1], wv[...])
    direct[...] = grad
    keep = 1.0 - flags[START].astype(F32)
    work[...] = keep * (forget[...] * cotangent[...] + grad)
    own[...] = work[pl.ds(pl.multiple_of(flags[CORE] * HALF, HALF), HALF)].astype(BF)
    give[...] = work[pl.ds(pl.multiple_of((1 - flags[CORE]) * HALF, HALF), HALF)].astype(BF)


def direct_grad(clock, state_grad, wk, wv, forget, cotangent):
    step = 256
    row = pl.BlockSpec((step, D), lambda j, *_: (j, 0))
    column = pl.BlockSpec((NS, step), lambda j, *_: (0, j))
    half = pl.BlockSpec((HALF, step), lambda j, *_: (0, j))
    return clock.run(
        direct_kernel,
        (shape((NS, D), F32), shape((HALF, D), BF), shape((HALF, D), BF)),
        (state_grad, wk, wv, forget, cotangent),
        (D // step,),
        [whole((2, NS, D)), row, row, column, column],
        (column, half, half),
        [pltpu.VMEM((NS, step), F32)],
        flops=4 * NS * D * D,
    )


def state_back_kernel(
    flags,
    mine,
    other,
    cotangent,
    forget,
    update,
    state_in,
    direct,
    wu,
    wg,
    initial_grad,
    projected_grad,
    bias_grad,
    summary_grad,
    work,
    total,
):
    step = pl.program_id(0)
    for core, came in ((flags[CORE], mine), (1 - flags[CORE], other)):
        work[pl.ds(pl.multiple_of(core * HALF, HALF), HALF)] = came[...].astype(F32)
    out_grad = cotangent[...] + work[...]
    gate = forget[...]
    start = flags[START].astype(F32)
    initial_grad[...] = (start * (gate * out_grad + direct[...])).astype(BF)
    rest = 1.0 - gate
    gate_grad = out_grad * (state_in[...] - update[...]) * gate * rest
    bias_grad[...] = jnp.sum(gate_grad, axis=0, keepdims=True)
    fresh_grad = (out_grad * rest).astype(BF)
    gate_low = gate_grad.astype(BF)
    projected_grad[0] = fresh_grad
    projected_grad[1] = gate_low
    part = product_nt(fresh_grad, wu[...]) + product_nt(gate_low, wg[...])

    @pl.when(step == 0)
    def _():
        total[...] = part

    @pl.when(step > 0)
    def _():
        total[...] += part

    @pl.when(step == pl.num_programs(0) - 1)
    def _():
        summary_grad[...] = total[...].astype(BF)


def state_back(clock, mine, other, cotangent, forget, update, state_in, direct, state_weight):
    step = 256
    column = pl.BlockSpec((NS, step), lambda j, *_: (0, j))
    half = pl.BlockSpec((HALF, step), lambda j, *_: (0, j))
    return clock.run(
        state_back_kernel,
        (
            shape((NS, D), BF),
            shape((2, NS, D), BF),
            shape((1, D), F32),
            shape((NS, D), BF),
        ),
        (mine, other, cotangent, forget, update, state_in, direct, state_weight, state_weight),
        (D // step,),
        [half, half, column, column, column, column, column]
        + [
            pl.BlockSpec((D, step), lambda j, *_: (0, j)),
            pl.BlockSpec((D, step), lambda j, *_: (0, j + D // step)),
        ],
        (
            column,
            pl.BlockSpec((2, NS, step), lambda j, *_: (0, 0, j)),
            pl.BlockSpec((1, step), lambda j, *_: (0, j)),
            whole((NS, D)),
        ),
        [pltpu.VMEM((NS, step), F32), pltpu.VMEM((NS, D), F32)],
        flops=4 * NS * D * D,
    )


def summary_back_kernel(flags, *refs):
    for _, (asks, pair, grad, own_grad, asks_grad, pair_total) in each_head(*refs):
        queries, out_grad = asks[...], grad[...]
        expos, total = summary_probs_of(pair[0], queries)
        probs = expos * (1.0 / total)
        prob_grad = product_nt(pair[1], out_grad)
        rowdot = jnp.sum(probs * prob_grad, axis=0, keepdims=True)
        score_grad = (probs * (prob_grad - rowdot)).astype(BF)
        asks_grad[...] = (product_tn(pair[0], score_grad) * SCALE).T.astype(BF)
        pair_total[0] = (own_grad[0] + product(score_grad, queries) * SCALE).astype(BF)
        pair_total[1] = (own_grad[1] + product(probs.astype(BF), out_grad)).astype(BF)


def summary_back(clock, asks, pair, grad, own_grad):
    head = pl.BlockSpec((W, HEADS_WIDE), lambda h, *_: (0, h))
    both = pl.BlockSpec((2, W, HEADS_WIDE), lambda h, *_: (0, 0, h))
    return clock.run(
        summary_back_kernel,
        (shape((NS, D), BF), shape((2, W, D), BF)),
        (asks, pair, grad, own_grad),
        (HEADS // PER_STEP,),
        [head, both, head, both],
        (head, both),
        flops=10 * NS * W * D,
        stream=True,
    )


def tokens_back_kernel(
    flags,
    queries_grad,
    pair_total,
    returned,
    wq,
    wk,
    wv,
    tokens,
    gain,
    hidden_grad,
    tokens_grad,
    gain_grad,
    total,
):
    step = pl.program_id(0)

    @pl.when(step < 2)
    def _():
        part = product_nt(queries_grad[...], wq[...])
        total[...] = jnp.where(step == 0, part, total[...] + part)

    @pl.when((step >= 2) & (step < 4))
    def _():
        total[...] += product_nt(add_low(pair_total[0], returned[0]), wk[...])

    @pl.when(step >= 4)
    def _():
        total[...] += product_nt(add_low(pair_total[0], returned[0]), wv[...])

    @pl.when(step == 5)
    def _():
        inputs = tokens[...].astype(F32)
        scaled = rms_scale(inputs)
        grad = total[...]
        gain_grad[...] = jnp.sum(grad * inputs * scaled, axis=0, keepdims=True)
        weighted = grad * gain[...]
        tokens_grad[...] = (
            hidden_grad[...]
            + scaled * weighted
            - inputs
            * (scaled * scaled * scaled * jnp.mean(weighted * inputs, axis=-1, keepdims=True))
        )


def tokens_back(clock, queries_grad, pair_total, returned, wq, wk, wv, tokens, gain, hidden_grad):
    step = D // 2
    clamp = lambda i, low: jnp.clip(i - low, 0, 1)
    weight = lambda low: pl.BlockSpec((D, step), lambda i, *_: (0, clamp(i, low)))
    later = lambda i: jnp.maximum(i - 2, 0)
    pair = pl.BlockSpec((1, W, step), lambda i, *_: (later(i) // 2, 0, later(i) % 2))
    return clock.run(
        tokens_back_kernel,
        (shape((W, D), F32), shape((1, D), F32)),
        (queries_grad, pair_total, returned, wq, wk, wv, tokens, gain, hidden_grad),
        (6,),
        [
            pl.BlockSpec((W, step), lambda i, *_: (0, clamp(i, 0))),
            pair,
            pair,
            weight(0),
            weight(2),
            weight(4),
            fixed((W, D)),
            fixed((1, D)),
            fixed((W, D)),
        ],
        (whole((W, D)), whole((1, D))),
        [pltpu.VMEM((W, D), F32)],
        flops=6 * W * D * D,
    )


def chunk_natural(flags, place):
    return place


def chunk_along_x(flags, place):
    x = flags[CHIP] & 1
    return 2 * (place % 2) + (1 - x if place < 2 else x)


def chunk_along_y(flags, place):
    y = flags[CHIP] >> 1
    return 2 * (1 - y if place < 2 else y) + place % 2


def column_blocks(terms):
    return terms[0][1][0][0].shape[2] // D


def weight_kernel(plan, merge, flags, *refs):
    refs = list(refs)
    lefts = [refs.pop(0) for _ in range(plan["lefts"])]
    rights = [[refs.pop(0) for _ in adds] for adds in plan["rights"]]
    extras = [refs.pop(0) for _ in range(plan["extras"])]
    recv = refs.pop(0) if merge else None
    work = refs.pop()
    core = flags[CORE] if merge else 1 - flags[CORE]
    step, base, start = pl.program_id(0), 0, 0

    def write(along, place, at, here, part):
        rows = part.shape[0]
        if merge:
            chunk = (chunk_along_x, chunk_along_y)[along](flags, place)
            part = part.astype(F32) + recv[chunk, at : at + rows].astype(F32)
            refs[2 * along + place // 2][place % 2, here : here + rows] = part.astype(BF)
        else:
            refs[0][place, at : at + rows] = part.astype(BF)

    def source(along, place):
        chunk_of = (chunk_along_x, chunk_along_y)[along] if merge else chunk_natural
        return 2 * chunk_of(flags, place) + core

    for along, group in enumerate(plan["grads"]):
        here = 0
        for rows, blocks, terms in group:

            @pl.when(step == base)
            def _():
                for term, (left, _) in enumerate(terms):
                    for place in range(4):
                        first = pl.multiple_of(source(along, place) * rows, rows)
                        block = lefts[left][:, pl.ds(first, rows)]
                        work[term, place * rows : (place + 1) * rows] = block.T

            for block in range(blocks):

                @pl.when(step == base + block)
                def _():
                    total = 0.0
                    for term, (_, right) in enumerate(terms):
                        parts = [part[0] for part in rights[right]]
                        value = parts[0] if len(parts) == 1 else add_low(*parts)
                        total = total + product(work[term, : 4 * rows], value)
                    at = block * rows
                    for place in range(4):
                        part = total[place * rows : (place + 1) * rows]
                        write(along, place, start + at, here + at, part)

            base += blocks
            start += blocks * rows
            here += blocks * rows
        if extras:
            rows = extras[along].shape[0] // 8

            @pl.when(step == 0)
            def _():
                for place in range(4):
                    first = pl.multiple_of(source(along, place) * rows, rows)
                    write(along, place, start, here, extras[along][pl.ds(first, rows)])

            start += rows


def weight_pair(clock, grads, extras, recv):
    lefts, left_ids, rights, args, specs, plans = [], {}, [], [], [], []
    base, start, tokens, most = 0, 0, grads[0][0][0][0].shape[0], 0
    sizes = []
    for along, group in enumerate(grads):
        total, plan = 0, []
        for terms in group:
            rows, blocks = terms[0][0].shape[1] // 8, column_blocks(terms)
            most = max(most, rows)
            steps = []
            for left, adds in terms:
                if id(left) not in left_ids:
                    left_ids[id(left)] = len(lefts)
                    lefts.append(left)
                steps.append((left_ids[id(left)], len(rights)))
                rights.append(tuple(index for _, index in adds))
                for right, index in adds:
                    args.append(right)
                    specs.append(
                        pl.BlockSpec(
                            (1, tokens, D),
                            lambda j, *_, index=index, base=base, blocks=blocks: (
                                index,
                                0,
                                jnp.clip(j - base, 0, blocks - 1),
                            ),
                        )
                    )
            plan.append((rows, blocks, steps))
            base += blocks
            total += blocks * rows
        if extras:
            total += extras[along].shape[0] // 8
        plans.append(plan)
        sizes.append(total)
        start += total
    args = lefts + args + list(extras)
    specs = [fixed(left.shape) for left in lefts] + specs + [fixed(e.shape) for e in extras]
    merge = recv is not None
    if merge:
        args.append(recv)
        specs.append(fixed(recv.shape))
        dims = [(2, total, D) for total in sizes for _ in range(2)]
    else:
        dims = [(4, start, D)]
    plan = {"lefts": len(lefts), "rights": rights, "extras": len(extras), "grads": plans}
    return clock.run(
        functools.partial(weight_kernel, plan, merge),
        tuple(shape(d, BF) for d in dims),
        tuple(args),
        (base,),
        specs,
        tuple(whole(d) for d in dims),
        [pltpu.VMEM((len(grads[0][0]), 4 * most, tokens), BF)],
        flops=2 * tokens * 4 * start * D * len(grads[0][0]),
        limit=24,
    )


def scatter_bits(value, bits, names):
    place = lax.axis_index("seq")
    names = list(names)
    for bit in bits:
        at = names.index(bit)
        mine = (place >> bit) & 1
        recv = swapped(pick(value, 1 - mine, at), "seq", 1 << bit)
        value = add_low(pick(value, mine, at), recv)
        names.pop(at)
    return value


def whole_scatter(value, along_x):
    count = lax.axis_size("seq")
    levels = count.bit_length() - 1
    names = list(range(levels - 1, -1, -1))
    value = value.reshape((2,) * levels + (value.shape[0] // count,) + value.shape[1:])
    bits = [0] + (names[-2::-1] if along_x else names[:-1])
    return scatter_bits(value, bits, names)


def in_rows(value):
    return jnp.concatenate([value[:, at : at + D] for at in range(0, value.shape[1], D)], axis=0)


def turn_kernel(flags, kept1, recv1, kept2, recv2, send1, send2):
    send1[...] = add_low(kept1[0], recv1[0])
    send2[...] = add_low(kept2[0], recv2[0])


def pack_kernel(flags, *refs):
    out, start = refs[-1], 0
    for at in range(0, len(refs) - 1, 3):
        kept, recv, last = refs[at : at + 3]
        rows = last.shape[0]
        out[start : start + rows] = add_low(kept[0], recv[0], last[...])
        start += rows


class Scatter:
    def __init__(self, clock, firsts, seconds, extras=()):
        self.grads, self.extras, self.plain = (firsts, seconds), extras, None
        if lax.axis_size("seq") != 8:
            sums = []
            for number, group in enumerate(self.grads):
                for terms in group:
                    total = 0.0
                    for left, adds in terms:
                        parts = [right[index] for right, index in adds]
                        right = add_low(*parts) if len(parts) > 1 else parts[0]
                        total = total + product_tn(left, right)
                    sums.append(in_rows(whole_scatter(total.astype(BF), number == 0)))
                if extras:
                    sums.append(whole_scatter(extras[number], number == 0))
            self.plain = jnp.concatenate(sums, axis=0)
            return
        (self.give,) = weight_pair(clock, self.grads, self.extras, None)

    def core(self, clock):
        if self.plain is None:
            self.recv = swapped(clock.at(self.give), "seq", 1)

    def keep(self, clock):
        if self.plain is None:
            send1, kept1, send2, kept2 = weight_pair(clock, self.grads, self.extras, self.recv)
            self.kept, self.send = (kept1, kept2), (send1, send2)

    def near(self, clock):
        if self.plain is None:
            self.recv = tuple(
                swapped(clock.at(send), "seq", far) for send, far in zip(self.send, (2, 4))
            )

    def held(self, other):
        args, specs = [], []
        for number, (kept, recv) in enumerate(zip(self.kept, self.recv)):
            bit = 1 - number
            mine = lambda i, flags, bit=bit: (((flags[CHIP] >> bit) & 1) ^ other, 0, 0)
            args.append([kept, recv])
            specs.append([pl.BlockSpec((1,) + kept.shape[1:], mine)] * 2)
        return args, specs

    def turn(self, clock, flops=0):
        if self.plain is None:
            args, specs = self.held(1)
            dims = [kept.shape[1:] for kept in self.kept]
            self.send = clock.run(
                turn_kernel,
                tuple(shape(d, BF) for d in dims),
                tuple(args[0] + args[1]),
                (1,),
                specs[0] + specs[1],
                tuple(whole(d) for d in dims),
                flops=flops,
                limit=10,
            )

    def far(self, clock):
        if self.plain is None:
            self.last = tuple(
                swapped(clock.at(send), "seq", far) for send, far in zip(self.send, (4, 2))
            )

    def parts(self):
        args, specs = self.held(0)
        for number, last in enumerate(self.last):
            args[number].append(last)
            specs[number].append(whole(last.shape))
        return args[0] + args[1], specs[0] + specs[1]


def pack(clock, *scatters):
    if scatters[0].plain is not None:
        return jnp.concatenate([scatter.plain for scatter in scatters], axis=0)
    args, specs = [], []
    for scatter in scatters:
        more = scatter.parts()
        args += more[0]
        specs += more[1]
    total = sum(arg.shape[0] for arg in args[2::3])
    return clock.run(
        pack_kernel,
        (shape((total, D), BF),),
        tuple(args),
        (1,),
        specs,
        (whole((total, D)),),
        limit=16,
    )[0]


class Line:
    def __init__(self, clock, value):
        count = lax.axis_size("dp")
        half = count // 2
        self.value = value
        self.rounds = (
            [([(s, s + 1), (count - 1 - s, count - 2 - s)], None) for s in range(half - 1)]
            + [([(half - 1, half), (half, half - 1)], None)]
            + [
                ([(s + 1, s), (count - 2 - s, count - 1 - s)], (s, count - 1 - s))
                for s in range(half - 2, -1, -1)
            ]
        )
        self.send(clock)

    def send(self, clock):
        self.recv = lax.ppermute(clock.at(self.value), "dp", self.rounds[0][0])

    def take(self, clock):
        place = lax.axis_index("dp")
        takers = self.rounds.pop(0)[1]
        value = clock.at(self.value)
        if takers is None:
            self.value = add_low(value, self.recv)
        else:
            outer = (place == takers[0]) | (place == takers[1])
            self.value = jnp.where(outer, self.recv, value)
        if self.rounds:
            clock.after(self.value)

    def step(self, clock):
        self.take(clock)
        if self.rounds:
            self.send(clock)

    def finish(self, clock):
        while self.rounds:
            self.step(clock)
        return self.value.astype(F32)


def interleaved(first, second):
    blocks = []
    for at in range(0, first.shape[1], PIECE):
        blocks += [first[:, at : at + PIECE], second[:, at : at + PIECE]]
    return jnp.concatenate(blocks, axis=1)


def body(
    tokens,
    item_starts,
    attn_gain,
    query_weight,
    key_weight,
    value_weight,
    output_weight,
    state_queries,
    state_weight,
    gate_bias,
    initial_state,
    mlp_gain,
    up_weight,
    down_weight,
    out_cotangent,
    state_cotangent,
):
    count = lax.axis_size("seq")
    place = lax.axis_index("seq")
    clock = Clock(
        jnp.stack([item_starts[0, 0], place & 1, (place >> 1) & 3]).astype(jnp.int32)
    )
    tokens, cotangent, state_cot = tokens[0], out_cotangent[0], state_cotangent[0, 0]
    attn_gain, gate_bias, mlp_gain = attn_gain[None], gate_bias[None], mlp_gain[None]
    down_weight = down_weight.reshape(FF // (2 * PIECE), 2 * PIECE, D)

    tokens_left = shifted(tokens, "seq", 1)
    normed, queries, own = front(clock, tokens, attn_gain, query_weight, key_weight, value_weight)
    summary, forget, update, give_pair, own_pair = gates(
        clock, state_queries, own, state_weight, gate_bias, initial_state
    )
    recv_pair = swapped(give_pair, "seq", 1)
    left = left_pair(clock, tokens_left, attn_gain, key_weight, value_weight)
    kept_chips = compose(clock, own_pair, recv_pair)
    come1, come2 = come_back(clock, cotangent, down_weight)
    back = prefix(clock, kept_chips)
    mine, other = previous(clock, back, own_pair, recv_pair)
    state_in, state_low, state_out, state = state_pair(
        clock, mine, other, initial_state, forget, update, key_weight, value_weight
    )
    attended, lse = attend(clock, queries, left, own, state)
    split = count == 8
    activated1, upper_grad1, normed_mlp, hidden, total, grad = mlp_first(
        clock, attended, tokens, output_weight, mlp_gain, come1, up_weight, down_weight
    )
    out_grads = (cotangent[None], 0)
    if split:
        feed1 = Scatter(
            clock,
            [[(activated1, [out_grads])]],
            [[(normed_mlp, [(upper_grad1[None], 0)])]],
        )
        feed1.core(clock)
        feed1.keep(clock)
        feed1.near(clock)
    activated2, upper_grad2, mixed, hidden_grad, attended_grad, heads_grad, mlp_gain_grad = (
        mlp_second(
            clock,
            normed_mlp,
            hidden,
            total,
            grad,
            output_weight,
            mlp_gain,
            cotangent,
            come2,
            up_weight,
            down_weight,
        )
    )
    if split:
        feed2 = Scatter(
            clock,
            [[(activated2, [out_grads])]],
            [[(normed_mlp, [(upper_grad2[None], 0)])]],
        )
        feed2.core(clock)
        feed1.turn(clock, LONG)
        feed1.far(clock)
        feed2.keep(clock)
        feed2.near(clock)
    else:
        feed1 = Scatter(
            clock,
            [[(interleaved(activated1, activated2), [out_grads])]],
            [[(normed_mlp, [(interleaved(upper_grad1, upper_grad2)[None], 0)])]],
        )
    queries_grad, left_grad, own_grad, state_grad = attend_back(
        clock, queries, left, own, state, heads_grad, lse
    )
    direct, own_base, give_base = direct_grad(
        clock, state_grad, key_weight, value_weight, forget, state_cot
    )
    recv_base = swapped(give_base, "seq", 1)
    line1 = Line(clock, pack(clock, feed1))
    got = compose_back(clock, own_base, recv_base, own_pair, recv_pair)
    if split:
        feed2.turn(clock)
    back = suffix(clock, got, kept_chips)
    mine, other = following(clock, back, own_base, recv_base, own_pair, recv_pair)
    if split:
        feed2.far(clock)
    returned = shifted(clock.at(left_grad), "seq", -1)
    line1.step(clock)
    initial_grad, projected_grad, gate_bias_grad, summary_grad = state_back(
        clock, mine, other, state_cot, forget, update, state_in, direct, state_weight
    )
    others = Scatter(
        clock,
        [[(attended, [(attended_grad[None], 0)])], [(summary, [(projected_grad, 0)])]],
        [[(normed, [(queries_grad[None], 0)])], [(summary, [(projected_grad, 1)])]],
    )
    line2 = Line(clock, pack(clock, feed2)) if split else None
    others.core(clock)
    state_queries_grad, pair_total = summary_back(
        clock, state_queries, own, summary_grad, own_grad
    )
    others.keep(clock)
    if split:
        line2.step(clock)
    others.near(clock)
    line1.take(clock)
    keys_values = Scatter(
        clock,
        [[(normed, [(pair_total, 0), (returned, 0)]), (state_low, [(state_grad, 0)])]],
        [[(normed, [(pair_total, 1), (returned, 1)]), (state_low, [(state_grad, 1)])]],
        (state_queries_grad, initial_grad),
    )
    keys_values.core(clock)
    if line1.rounds:
        line1.send(clock)
    keys_values.keep(clock)
    if split:
        line2.take(clock)
    keys_values.near(clock)
    tokens_grad, attn_gain_grad = tokens_back(
        clock,
        queries_grad,
        pair_total,
        returned,
        query_weight,
        key_weight,
        value_weight,
        tokens,
        attn_gain,
        hidden_grad,
    )
    others.turn(clock)
    others.far(clock)
    line1 = line1.finish(clock)
    clock.after(line1)
    lanes, rows = D // count, NS // count
    vectors = jnp.concatenate([attn_gain_grad, gate_bias_grad, mlp_gain_grad])
    vectors = vectors.reshape(3, count, lanes).transpose(1, 0, 2).reshape(count, 1, 3 * lanes)
    vectors = jnp.pad(vectors, ((0, 0), (0, 7), (0, D - 3 * lanes))).astype(BF)
    keys_values.turn(clock)
    keys_values.far(clock)
    vectors = whole_scatter(clock.at(vectors.reshape(-1, D)), True)
    line3 = [Line(clock, half) for half in jnp.split(pack(clock, others), 2)]
    if split:
        line2.send(clock)
    line4 = Line(clock, jnp.concatenate([pack(clock, keys_values), vectors], axis=0))
    for line in line3 + [line4] + line3 + [line4]:
        line.step(clock)
    line3 = [line.finish(clock) for line in line3]
    line4 = line4.finish(clock)
    clock.after(line3, line4)
    line2 = line2.finish(clock) if split else None

    def unpack(packed, *dims):
        pieces, start = [], 0
        for high, wide in dims:
            parts = [
                packed[start + high * part : start + high * (part + 1)] for part in range(wide // D)
            ]
            start += high * (wide // D)
            pieces.append(parts[0] if len(parts) == 1 else jnp.concatenate(parts, axis=1))
        return pieces

    high, deep = D // count, FF // count
    if split:
        down1, up1 = unpack(line1, (deep // 2, D), (high, FF // 2))
        down2, up2 = unpack(line2, (deep // 2, D), (high, FF // 2))
        down_grad = jnp.concatenate([down1, down2], axis=0)
        up_grad = interleaved(up1, up2)
    else:
        down_grad, up_grad = unpack(line1, (deep, D), (high, FF))
    output_grad, first_grad, query_grad, second_grad = unpack(
        jnp.concatenate(line3),
        (high, D),
        (high, D),
        (high, D),
        (high, D),
    )
    state_weight_grad = jnp.concatenate([first_grad, second_grad], axis=1)
    key_grad, state_queries_grad, value_grad, initial_grad, vectors = unpack(
        line4, (high, D), (rows, D), (high, D), (rows, D), (8, D)
    )
    vectors = vectors[0, : 3 * lanes]
    return (
        mixed[None],
        state_out[None, None],
        tokens_grad[None],
        vectors[:lanes],
        query_grad,
        key_grad,
        value_grad,
        output_grad,
        state_queries_grad,
        state_weight_grad,
        vectors[lanes : 2 * lanes],
        initial_grad,
        vectors[2 * lanes :],
        up_grad,
        down_grad,
    )


def solution(mesh):
    in_specs = (
        P("dp", "seq", None),
        P("dp", "seq"),
        P(),
        P(),
        P(),
        P(),
        P(),
        P(),
        P(),
        P(),
        P(),
        P(),
        P(),
        P(),
        P("dp", "seq", None),
        P("dp", "seq", None, None),
    )
    out_specs = (
        P("dp", "seq", None),
        P("dp", "seq", None, None),
        P("dp", "seq", None),
        P("seq"),
        P("seq", None),
        P("seq", None),
        P("seq", None),
        P("seq", None),
        P("seq", None),
        P("seq", None),
        P("seq"),
        P("seq", None),
        P("seq"),
        P("seq", None),
        P("seq", None),
    )
    return jax.shard_map(body, mesh=mesh, in_specs=in_specs, out_specs=out_specs, check_vma=False)
```

profile of v0, /device:TPU:0, one launch (start us, length us, event | category | flops | bytes accessed | tf_op | source)
XLA Modules:
  0.0 428.1 jit_solution(752498273054804934)
XLA Ops:
  5.7 7.3 %shard_map.271 = (bf16[512,1024]{1,0:T(8,128)(2,1)S(1)}, bf16[512,1024]{1,0:T(8,128)(2,1)S(1)}, bf16[2,512,1024]{2,1,0:T(8,128)(2,1)S(1)}) custom-call(s32[3]{0:T(128)S(1)} %pad_add_fusion.flags, bf16[512,1024]{1,0:T(8,128)(2,1)S(1)} %bitcast.72, f32[1,1024]{1,0:T(1,128)S(1)} %bitcast.80, bf16[1024,1024]{1,0:T(8,128)(2,1)} %wq.3, bf16[1024,1024]{1,0:T(8,128)(2,1)} %wk.9, ...), custom_call_target="tpu_custom_call" | custom-call | flops 3221225472 | bytes 11538432 | tf_op jit(solution)/shard_map/pallas_call | solution.py:103
  14.1 10.9 %shard_map.272 = (bf16[512,1024]{1,0:T(8,128)(2,1)S(1)}, f32[512,1024]{1,0:T(8,128)S(1)}, f32[512,1024]{1,0:T(8,128)S(1)}, bf16[2,256,1024]{2,1,0:T(8,128)(2,1)S(1)}, bf16[2,256,1024]{2,1,0:T(8,128)(2,1)S(1)}) custom-call(s32[3]{0:T(128)S(1)} %pad_add_fusion.flags, bf16[512,1024]{1,0:T(8,128)(2,1)S(1)} %copy-done.67, ...), custom_call_target="tpu_custom_call" | custom-call | flops 3221225472 | bytes 20975616 | tf_op jit(solution)/shard_map/pallas_call | solution.py:103
  27.6 4.6 %shard_map.273.refs_1_.left = bf16[2,512,1024]{2,1,0:T(8,128)(2,1)S(1)} custom-call(s32[3]{0:T(128)S(1)} %pad_add_fusion.flags, bf16[512,1024]{1,0:T(8,128)(2,1)S(1)} %collective-permute-done.tokens, f32[1,1024]{1,0:T(1,128)S(1)} %bitcast.81, bf16[1024,1024]{1,0:T(8,128)(2,1)S(1)} %copy-done.8, bf16[1024,1024]{1,0:T(8,128)(2,1)S(1)} %copy-done.11), custom_call_target="tpu_custom_call" | custom-call | flops 99999997952 | bytes 7344128 | tf_op jit(solution)/shard_map/pallas_call | solution.py:103
  38.6 6.6 %shard_map.275 = (bf16[512,2048]{1,0:T(8,128)(2,1)S(1)}, bf16[512,2048]{1,0:T(8,128)(2,1)S(1)}) custom-call(s32[3]{0:T(128)S(1)} %pad_add_fusion.flags, bf16[512,1024]{1,0:T(8,128)(2,1)S(1)} %bitcast.61, bf16[8,512,1024]{2,1,0:T(8,128)(2,1)S(1)} %bitcast.59, bf16[8,512,1024]{2,1,0:T(8,128)(2,1)S(1)} %bitcast.60), custom_call_target="tpu_custom_call" | custom-call | flops 4294967296 | bytes 22020096 | tf_op jit(solution)/shard_map/pallas_call | solution.py:103
  45.2 5.0 %collective-permute-done.3.from2.kept2 = bf16[2,64,1024]{2,1,0:T(8,128)(2,1)S(1)} collective-permute-done((bf16[2,64,1024]{2,1,0:T(8,128)(2,1)S(1)}, bf16[2,64,1024]{2,1,0:T(8,128)(2,1)S(1)}, u32[]{:S(2)}, u32[]{:S(2)}) %collective-permute-start.3) | collective-permute-done | bytes 262176 | tf_op jit(solution)/shard_map/ppermute | solution.py:35
  62.7 5.5 %shard_map.278 = (f32[512,1024]{1,0:T(8,128)S(1)}, bf16[512,1024]{1,0:T(8,128)(2,1)S(1)}, f32[512,1024]{1,0:T(8,128)}, bf16[2,512,1024]{2,1,0:T(8,128)(2,1)S(1)}) custom-call(s32[3]{0:T(128)S(1)} %pad_add_fusion.flags, bf16[256,1024]{1,0:T(8,128)(2,1)S(1)} %get-tuple-element.219.mine, bf16[256,1024]{1,0:T(8,128)(2,1)S(1)} %collective-permute-done.8.other, ...), custom_call_target="tpu_custom_call" | custom-call | flops 2147483648 | bytes 18874368 | tf_op jit(solution)/shard_map/pallas_call | solution.py:103
  69.5 14.3 %shard_map.279 = (bf16[512,1024]{1,0:T(8,128)(2,1)S(1)}, f32[8,1,512]{2,1,0:T(1,128)S(1)}) custom-call(s32[3]{0:T(128)S(1)} %pad_add_fusion.flags, bf16[512,1024]{1,0:T(8,128)(2,1)} %copy-done.98, bf16[2,512,1024]{2,1,0:T(8,128)(2,1)} %copy-done.97, bf16[2,512,1024]{2,1,0:T(8,128)(2,1)} %copy-done.57, bf16[2,512,1024]{2,1,0:T(8,128)(2,1)} %copy-done.91), custom_call_target="tpu_custom_call" | custom-call | flops 3221225472 | bytes 8404992 | tf_op jit(solution)/shard_map/pallas_call | solution.py:103
  83.8 13.4 %shard_map.280 = (bf16[512,2048]{1,0:T(8,128)(2,1)S(1)}, bf16[512,2048]{1,0:T(8,128)(2,1)S(1)}, bf16[512,1024]{1,0:T(8,128)(2,1)S(1)}, f32[512,1024]{1,0:T(8,128...) custom-call(s32[3]{0:T(128)S(1)} %pad_add_fusion.flags, ...), custom_call_target="tpu_custom_call" | custom-call | flops 7516192768 | bytes 42995712 | tf_op jit(solution)/shard_map/pallas_call | solution.py:103
  99.9 3.6 shard_map.281
  103.7 7.0 %collective-permute-done.9.refs_4_ = bf16[4,512,1024]{2,1,0:T(8,128)(2,1)S(1)} collective-permute-done((bf16[4,512,1024]{2,1,0:T(8,128)(2,1)S(1)}, bf16[4,512,1024]{2,1,0:T(8,128)(2,1)S(1)}, u32[]{:S(2)}, u32[]{:S(2)}) %collective-permute-start.9) | collective-permute-done | bytes 4194336 | tf_op jit(solution)/shard_map/ppermute | solution.py:35
  110.7 4.9 %shard_map.282 = (bf16[2,256,1024]{2,1,0:T(8,128)(2,1)}, bf16[2,256,1024]{2,1,0:T(8,128)(2,1)S(1)}, bf16[2,256,1024]{2,1,0:T(8,128)(2,1)}, bf16[2,256,1024]{2,1,0:T(8,128)(2,1)S(1)}) custom-call(s32[3]{0:T(128)S(1)} %pad_add_fusion.flags, bf16[512,2048]{1,0:T(8,128)(2,1)S(1)} %get-tuple-element.230.refs_0_, ...), custom_call_target="tpu_custom_call" | custom-call | flops 2147483648 | bytes 14680064 | tf_op jit(solution)/shard_map/pallas_call | solution.py:103
  122.8 15.9 %shard_map.283 = (bf16[512,2048]{1,0:T(8,128)(2,1)S(1)}, bf16[512,2048]{1,0:T(8,128)(2,1)S(1)}, bf16[512,1024]{1,0:T(8,128)(2,1)}, f32[512,1024]{1,0:T(8,128)S(1...) custom-call(s32[3]{0:T(128)S(1)} %pad_add_fusion.flags, ...), custom_call_target="tpu_custom_call" | custom-call | flops 7516192768 | bytes 47194112 | tf_op jit(solution)/shard_map/pallas_call | solution.py:103
  138.7 3.6 shard_map.284
  149.5 5.0 %shard_map.286 = (bf16[2,256,1024]{2,1,0:T(8,128)(2,1)}, bf16[2,256,1024]{2,1,0:T(8,128)(2,1)S(1)}, bf16[2,256,1024]{2,1,0:T(8,128)(2,1)}, bf16[2,256,1024]{2,1,0:T(8,128)(2,1)S(1)}) custom-call(s32[3]{0:T(128)S(1)} %pad_add_fusion.flags, bf16[512,2048]{1,0:T(8,128)(2,1)S(1)} %get-tuple-element.244.refs_0_, ...), custom_call_target="tpu_custom_call" | custom-call | flops 2147483648 | bytes 14680064 | tf_op jit(solution)/shard_map/pallas_call | solution.py:103
  156.6 23.0 %shard_map.287 = (bf16[512,1024]{1,0:T(8,128)(2,1)S(1)}, bf16[2,512,1024]{2,1,0:T(8,128)(2,1)S(1)}, f32[2,512,1024]{2,1,0:T(8,128)S(1)}, bf16[2,512,1024]{2,1,0:T(8,128)(2,1)S(1)}) custom-call(s32[3]{0:T(128)S(1)} %pad_add_fusion.flags, bf16[512,1024]{1,0:T(8,128)(2,1)} %copy-done.98, bf16[2,512,1024]{2,1,0:T(8,128)(2,1)} %copy-done.97, ...), custom_call_target="tpu_custom_call" | custom-call | flops 8053063680 | bytes 17842176 | tf_op jit(solution)/shard_map/pallas_call | solution.py:103
  179.7 4.3 %shard_map.288 = (f32[512,1024]{1,0:T(8,128)S(1)}, bf16[256,1024]{1,0:T(8,128)(2,1)S(1)}, bf16[256,1024]{1,0:T(8,128)(2,1)S(1)}) custom-call(s32[3]{0:T(128)S(1)} %pad_add_fusion.flags, bf16[2,512,1024]{2,1,0:T(8,128)(2,1)S(1)} %get-tuple-element.262.state_grad.refs_4_.refs_7_, bf16[1024,1024]{1,0:T(8,128)(2,1)S(1)} %copy-done.9, ...), custom_call_target="tpu_custom_call" | custom-call | flops 2147483648 | bytes 13631488 | tf_op jit(solution)/shard_map/pallas_call | solution.py:103
  215.6 6.9 %shard_map.294 = (bf16[512,1024]{1,0:T(8,128)(2,1)S(1)}, bf16[2,512,1024]{2,1,0:T(8,128)(2,1)S(1)}, f32[1,1024]{1,0:T(1,128)S(1)}, bf16[512,1024]{1,0:T(8,128)(2,1)S(1)}) custom-call(s32[3]{0:T(128)S(1)} %pad_add_fusion.flags, bf16[256,1024]{1,0:T(8,128)(2,1)S(1)} %get-tuple-element.288.mine, bf16[256,1024]{1,0:T(8,128)(2,1)S(1)} %collective-permute-done.25.other, ...), custom_call_target="tpu_custom_call" | custom-call | flops 2147483648 | bytes 24121344 | tf_op jit(solution)/shard_map/pallas_call | solution.py:103
  222.5 3.7 shard_map.295
  232.4 12.3 %shard_map.297 = (bf16[512,1024]{1,0:T(8,128)(2,1)S(1)}, bf16[2,512,1024]{2,1,0:T(8,128)(2,1)S(1)}) custom-call(s32[3]{0:T(128)S(1)} %pad_add_fusion.flags, bf16[512,1024]{1,0:T(8,128)(2,1)} %refs_0_.1, bf16[2,512,1024]{2,1,0:T(8,128)(2,1)} %copy-done.57, bf16[512,1024]{1,0:T(8,128)(2,1)} %copy-done.93, f32[2,512,1024]{2,1,0:T(8,128)} %copy-done.96), custom_call_target="tpu_custom_call" | custom-call | flops 2684354560 | bytes 11534336 | tf_op jit(solution)/shard_map/pallas_call | solution.py:103
  249.3 5.1 %shard_map.298 = (bf16[2,256,1024]{2,1,0:T(8,128)(2,1)}, bf16[2,256,1024]{2,1,0:T(8,128)(2,1)S(1)}, bf16[2,256,1024]{2,1,0:T(8,128)(2,1)}, bf16[2,256,1024]{2,1,0:T(8,128)(2,1)S(1)}) custom-call(s32[3]{0:T(128)S(1)} %pad_add_fusion.flags, bf16[512,1024]{1,0:T(8,128)(2,1)S(1)} %get-tuple-element.228.attended.refs_0_, bf16[512,1024]{1,0:T(8,128)(2,1)S(1)} %copy-done.45, ...), custom_call_target="tpu_custom_call" | custom-call | flops 2147483648 | bytes 17825792 | tf_op jit(solution)/shard_map/pallas_call | solution.py:103
  257.7 5.0 %shard_map.299 = bf16[4,384,1024]{2,1,0:T(8,128)(2,1)} custom-call(s32[3]{0:T(128)S(1)} %pad_add_fusion.flags, bf16[512,1024]{1,0:T(8,128)(2,1)S(1)} %get-tuple-element.199.refs_2_.refs_0_, bf16[512,1024]{1,0:T(8,128)(2,1)S(1)} %get-tuple-element.316.refs_1_, bf16[2,512,1024]{2,1,0:T(8,128)(2,1)S(1)} %get-tuple-element.317.refs_2_.refs_5_.pair_total, ...), custom_call_target="tpu_custom_call" | custom-call | flops 3221225472 | bytes 19922944 | tf_op jit(solution)/shard_map/pallas_call | solution.py:103
  276.4 6.0 %shard_map.300 = (bf16[2,192,1024]{2,1,0:T(8,128)(2,1)S(1)}, bf16[2,192,1024]{2,1,0:T(8,128)(2,1)S(1)}, bf16[2,192,1024]{2,1,0:T(8,128)(2,1)S(1)}, bf16[2,192,1024]{2,1,0:T(8,128)(2,1)S(1)}) custom-call(s32[3]{0:T(128)S(1)} %pad_add_fusion.flags, bf16[512,1024]{1,0:T(8,128)(2,1)S(1)} %get-tuple-element.199.refs_2_.refs_0_, bf16[512,1024]{1,0:T(8,128)(2,1)S(1)} %copy-done.31, ...), custom_call_target="tpu_custom_call" | custom-call | flops 3221225472 | bytes 23068672 | tf_op jit(solution)/shard_map/pallas_call | solution.py:103
  289.0 8.7 %shard_map.301 = (f32[512,1024]{1,0:T(8,128)}, f32[1,1024]{1,0:T(1,128)S(1)}) custom-call(s32[3]{0:T(128)S(1)} %pad_add_fusion.flags, bf16[512,1024]{1,0:T(8,128)(2,1)S(1)} %copy-done.21, bf16[2,512,1024]{2,1,0:T(8,128)(2,1)S(1)} %copy-done.4, bf16[2,512,1024]{2,1,0:T(8,128)(2,1)S(1)} %collective-permute-done.31.refs_3_.refs_6_.returned, ...), custom_call_target="tpu_custom_call" | custom-call | flops 3221225472 | bytes 16785408 | tf_op jit(solution)/shard_map/pallas_call | solution.py:103
  304.6 3.9 collective-permute-done.38.recv2.refs_4_
  313.2 7.7 %collective-permute-done.40.refs_5_ = bf16[256,1024]{1,0:T(8,128)(2,1)S(1)} collective-permute-done((bf16[256,1024]{1,0:T(8,128)(2,1)}, bf16[256,1024]{1,0:T(8,128)(2,1)S(1)}, u32[]{:S(2)}, u32[]{:S(2)}) %collective-permute-start.40) | collective-permute-done | bytes 524320 | tf_op jit(solution)/shard_map/ppermute | solution.py:35
  332.0 9.6 %collective-permute-start.46 = (bf16[256,1024]{1,0:T(8,128)(2,1)S(1)}, bf16[256,1024]{1,0:T(8,128)(2,1)S(1)}, u32[]{:S(2)}, u32[]{:S(2)}) collective-permute-start(bf16[256,1024]{1,0:T(8,128)(2,1)S(1)} %get-tuple-element.359), channel_id=1, source_target_pairs={{0,1},{3,2},{4,5},{7,6},{8,9},{11,10},{12,13},{15,14},{16,17},{19,... | collective-permute-start | bytes 1572872 | tf_op jit(solution)/shard_map/ppermute | solution.py:1202
  345.5 5.1 %collective-permute-start.47 = (bf16[256,1024]{1,0:T(8,128)(2,1)S(1)}, bf16[256,1024]{1,0:T(8,128)(2,1)S(1)}, u32[]{:S(2)}, u32[]{:S(2)}) collective-permute-start(bf16[256,1024]{1,0:T(8,128)(2,1)S(1)} %get-tuple-element.362), channel_id=1, source_target_pairs={{0,1},{3,2},{4,5},{7,6},{8,9},{11,10},{12,13},{15,14},{16,17},{19,... | collective-permute-start | bytes 1572872 | tf_op jit(solution)/shard_map/ppermute | solution.py:1202
  354.1 11.0 %collective-permute-done.47 = bf16[256,1024]{1,0:T(8,128)(2,1)S(1)} collective-permute-done((bf16[256,1024]{1,0:T(8,128)(2,1)S(1)}, bf16[256,1024]{1,0:T(8,128)(2,1)S(1)}, u32[]{:S(2)}, u32[]{:S(2)}) %collective-permute-start.47) | collective-permute-done | bytes 524320 | tf_op jit(solution)/shard_map/ppermute | solution.py:1202
  368.3 11.0 %collective-permute-done.48 = bf16[392,1024]{1,0:T(8,128)(2,1)S(1)} collective-permute-done((bf16[392,1024]{1,0:T(8,128)(2,1)S(1)}, bf16[392,1024]{1,0:T(8,128)(2,1)S(1)}, u32[]{:S(2)}, u32[]{:S(2)}) %collective-permute-start.48) | collective-permute-done | bytes 802848 | tf_op jit(solution)/shard_map/ppermute | solution.py:1202
  386.8 15.7 %collective-permute-done.53 = bf16[256,1024]{1,0:T(8,128)(2,1)S(1)} collective-permute-done((bf16[256,1024]{1,0:T(8,128)(2,1)S(1)}, bf16[256,1024]{1,0:T(8,128)(2,1)S(1)}, u32[]{:S(2)}, u32[]{:S(2)}) %collective-permute-start.53) | collective-permute-done | bytes 524320 | tf_op jit(solution)/shard_map/ppermute | solution.py:1202
  402.6 10.1 %collective-permute-done.54 = bf16[256,1024]{1,0:T(8,128)(2,1)S(1)} collective-permute-done((bf16[256,1024]{1,0:T(8,128)(2,1)S(1)}, bf16[256,1024]{1,0:T(8,128)(2,1)S(1)}, u32[]{:S(2)}, u32[]{:S(2)}) %collective-permute-start.54) | collective-permute-done | bytes 524320 | tf_op jit(solution)/shard_map/ppermute | solution.py:1202
  415.7 9.7 %collective-permute-done.52 = bf16[392,1024]{1,0:T(8,128)(2,1)S(1)} collective-permute-done((bf16[392,1024]{1,0:T(8,128)(2,1)S(1)}, bf16[392,1024]{1,0:T(8,128)(2,1)S(1)}, u32[]{:S(2)}, u32[]{:S(2)}) %collective-permute-start.52) | collective-permute-done | bytes 802848 | tf_op jit(solution)/shard_map/ppermute | solution.py:1202
  (390 shorter events, 158.8 us)
Async XLA Ops:
  0.6 27.0 %collective-permute-start = (bf16[512,1024]{1,0:T(8,128)(2,1)}, bf16[512,1024]{1,0:T(8,128)(2,1)S(1)}, u32[]{:S(2)}, u32[]{:S(2)}) collective-permute-start(bf16[512,1024]{1,0:T(8,128)(2,1)} %bitcast.71), channel_id=1, source_target_pairs={{0,4},{4,8},{8,12},{12,16},{16,20},{20,24},{24,28},{1,5},{5,9},{9,... | collective-permute-start | bytes 3145736 | tf_op jit(solution)/shard_map/ppermute | solution.py:41
  117.6 25.4 %collective-permute-start.11 = (bf16[2,256,1024]{2,1,0:T(8,128)(2,1)}, bf16[2,256,1024]{2,1,0:T(8,128)(2,1)S(1)}, u32[]{:S(2)}, u32[]{:S(2)}) collective-permute-start(bf16[2,256,1024]{2,1,0:T(8,128)(2,1)} %get-tuple-element.252), channel_id=1, source_target_pairs={{0,16},{4,20},{8,24},{12,28},{16,0},{20,4},{24,8},{28,12},{1,17},{... | collective-permute-start | bytes 3145736 | tf_op jit(solution)/shard_map/ppermute | solution.py:35
  118.7 25.1 %collective-permute-start.10 = (bf16[2,256,1024]{2,1,0:T(8,128)(2,1)}, bf16[2,256,1024]{2,1,0:T(8,128)(2,1)S(1)}, u32[]{:S(2)}, u32[]{:S(2)}) collective-permute-start(bf16[2,256,1024]{2,1,0:T(8,128)(2,1)} %get-tuple-element.249), channel_id=1, source_target_pairs={{0,8},{4,12},{8,0},{12,4},{16,24},{20,28},{24,16},{28,20},{1,9},{5... | collective-permute-start | bytes 3145736 | tf_op jit(solution)/shard_map/ppermute | solution.py:35
  145.5 38.6 %collective-permute-start.14 = (bf16[256,1024]{1,0:T(8,128)(2,1)}, bf16[256,1024]{1,0:T(8,128)(2,1)}, u32[]{:S(2)}, u32[]{:S(2)}) collective-permute-start(bf16[256,1024]{1,0:T(8,128)(2,1)} %get-tuple-element.267), channel_id=1, source_target_pairs={{0,8},{4,12},{8,0},{12,4},{16,24},{20,28},{24,16},{28,20},{1,9},{5... | collective-permute-start | bytes 1572872 | tf_op jit(solution)/shard_map/ppermute | solution.py:35
  146.5 37.6 %collective-permute-start.13 = (bf16[256,1024]{1,0:T(8,128)(2,1)}, bf16[256,1024]{1,0:T(8,128)(2,1)}, u32[]{:S(2)}, u32[]{:S(2)}) collective-permute-start(bf16[256,1024]{1,0:T(8,128)(2,1)} %get-tuple-element.265), channel_id=1, source_target_pairs={{0,16},{4,20},{8,24},{12,28},{16,0},{20,4},{24,8},{28,12},{1,17},{... | collective-permute-start | bytes 1572872 | tf_op jit(solution)/shard_map/ppermute | solution.py:35
  154.5 40.6 %collective-permute-start.17 = (bf16[2,256,1024]{2,1,0:T(8,128)(2,1)}, bf16[2,256,1024]{2,1,0:T(8,128)(2,1)S(1)}, u32[]{:S(2)}, u32[]{:S(2)}) collective-permute-start(bf16[2,256,1024]{2,1,0:T(8,128)(2,1)} %get-tuple-element.277), channel_id=1, source_target_pairs={{0,16},{4,20},{8,24},{12,28},{16,0},{20,4},{24,8},{28,12},{1,17},{... | collective-permute-start | bytes 3145736 | tf_op jit(solution)/shard_map/ppermute | solution.py:35
  155.3 41.2 %collective-permute-start.16 = (bf16[2,256,1024]{2,1,0:T(8,128)(2,1)}, bf16[2,256,1024]{2,1,0:T(8,128)(2,1)S(1)}, u32[]{:S(2)}, u32[]{:S(2)}) collective-permute-start(bf16[2,256,1024]{2,1,0:T(8,128)(2,1)} %get-tuple-element.274), channel_id=1, source_target_pairs={{0,8},{4,12},{8,0},{12,4},{16,24},{20,28},{24,16},{28,20},{1,9},{5... | collective-permute-start | bytes 3145736 | tf_op jit(solution)/shard_map/ppermute | solution.py:35
  186.3 28.9 %collective-permute-start.24 = (bf16[512,1024]{1,0:T(8,128)(2,1)S(1)}, bf16[512,1024]{1,0:T(8,128)(2,1)S(1)}, u32[]{:S(2)}, u32[]{:S(2)}) collective-permute-start(bf16[512,1024]{1,0:T(8,128)(2,1)S(1)} %shard_map.289), channel_id=1, source_target_pairs={{0,1},{3,2},{4,5},{7,6},{8,9},{11,10},{12,13},{15,14},{16,17},{19,... | collective-permute-start | bytes 3145736 | tf_op jit(solution)/shard_map/ppermute | solution.py:1202
  212.8 14.3 %collective-permute-start.27 = (bf16[256,1024]{1,0:T(8,128)(2,1)S(1)}, bf16[256,1024]{1,0:T(8,128)(2,1)S(1)}, u32[]{:S(2)}, u32[]{:S(2)}) collective-permute-start(bf16[256,1024]{1,0:T(8,128)(2,1)S(1)} %get-tuple-element.301), channel_id=1, source_target_pairs={{0,8},{4,12},{8,0},{12,4},{16,24},{20,28},{24,16},{28,20},{1,9},{5... | collective-permute-start | bytes 1572872 | tf_op jit(solution)/shard_map/ppermute | solution.py:35
  228.9 15.8 %collective-permute-start.28 = (bf16[4,512,1024]{2,1,0:T(8,128)(2,1)S(1)}, bf16[4,512,1024]{2,1,0:T(8,128)(2,1)S(1)}, u32[]{:S(2)}, u32[]{:S(2)}) collective-permute-start(bf16[4,512,1024]{2,1,0:T(8,128)(2,1)S(1)} %shard_map.295), channel_id=1, source_target_pairs={{0,4},{4,0},{8,12},{12,8},{16,20},{20,16},{24,28},{28,24},{1,5},{5... | collective-permute-start | bytes 12582920 | tf_op jit(solution)/shard_map/ppermute | solution.py:35
  229.0 28.6 %collective-permute-start.31 = (bf16[2,512,1024]{2,1,0:T(8,128)(2,1)S(1)}, bf16[2,512,1024]{2,1,0:T(8,128)(2,1)S(1)}, u32[]{:S(2)}, u32[]{:S(2)}) collective-permute-start(bf16[2,512,1024]{2,1,0:T(8,128)(2,1)S(1)} %copy-done.90), channel_id=1, source_target_pairs={{4,0},{8,4},{12,8},{16,12},{20,16},{24,20},{28,24},{5,1},{9,5},{13... | collective-permute-start | bytes 6291464 | tf_op jit(solution)/shard_map/ppermute | solution.py:41
  230.3 24.5 %collective-permute-start.29 = (bf16[512,1024]{1,0:T(8,128)(2,1)S(1)}, bf16[512,1024]{1,0:T(8,128)(2,1)S(1)}, u32[]{:S(2)}, u32[]{:S(2)}) collective-permute-start(bf16[512,1024]{1,0:T(8,128)(2,1)S(1)} %shard_map.296), channel_id=1, source_target_pairs={{0,1},{3,2},{4,5},{7,6},{8,9},{11,10},{12,13},{15,14},{16,17},{19,... | collective-permute-start | bytes 3145736 | tf_op jit(solution)/shard_map/ppermute | solution.py:1202
  231.7 24.5 %collective-permute-start.30 = (bf16[512,1024]{1,0:T(8,128)(2,1)S(1)}, bf16[512,1024]{1,0:T(8,128)(2,1)S(1)}, u32[]{:S(2)}, u32[]{:S(2)}) collective-permute-start(bf16[512,1024]{1,0:T(8,128)(2,1)S(1)} %add_convert_fusion.3), channel_id=1, source_target_pairs={{1,2},{2,1},{5,6},{6,5},{9,10},{10,9},{13,14},{14,13},{17,18},{18,... | collective-permute-start | bytes 3145736 | tf_op jit(solution)/shard_map/ppermute | solution.py:1202
  263.8 18.6 %collective-permute-start.33 = (bf16[512,1024]{1,0:T(8,128)(2,1)}, bf16[512,1024]{1,0:T(8,128)(2,1)}, u32[]{:S(2)}, u32[]{:S(2)}) collective-permute-start(bf16[512,1024]{1,0:T(8,128)(2,1)} %add_convert_fusion.2), channel_id=1, source_target_pairs={{1,2},{2,1},{5,6},{6,5},{9,10},{10,9},{13,14},{14,13},{17,18},{18,... | collective-permute-start | bytes 3145736 | tf_op jit(solution)/shard_map/ppermute | solution.py:1202
  265.4 32.3 %collective-permute-start.35 = (bf16[2,256,1024]{2,1,0:T(8,128)(2,1)}, bf16[2,256,1024]{2,1,0:T(8,128)(2,1)}, u32[]{:S(2)}, u32[]{:S(2)}) collective-permute-start(bf16[2,256,1024]{2,1,0:T(8,128)(2,1)} %get-tuple-element.334), channel_id=1, source_target_pairs={{0,16},{4,20},{8,24},{12,28},{16,0},{20,4},{24,8},{28,12},{1,17},{... | collective-permute-start | bytes 3145736 | tf_op jit(solution)/shard_map/ppermute | solution.py:35
  267.4 30.3 %collective-permute-start.34 = (bf16[2,256,1024]{2,1,0:T(8,128)(2,1)}, bf16[2,256,1024]{2,1,0:T(8,128)(2,1)}, u32[]{:S(2)}, u32[]{:S(2)}) collective-permute-start(bf16[2,256,1024]{2,1,0:T(8,128)(2,1)} %get-tuple-element.331), channel_id=1, source_target_pairs={{0,8},{4,12},{8,0},{12,4},{16,24},{20,28},{24,16},{28,20},{1,9},{5... | collective-permute-start | bytes 3145736 | tf_op jit(solution)/shard_map/ppermute | solution.py:35
  268.1 33.7 %collective-permute-start.36 = (bf16[512,1024]{1,0:T(8,128)(2,1)}, bf16[512,1024]{1,0:T(8,128)(2,1)}, u32[]{:S(2)}, u32[]{:S(2)}) collective-permute-start(bf16[512,1024]{1,0:T(8,128)(2,1)} %add_convert_fusion.1), channel_id=1, source_target_pairs={{1,0},{2,3},{5,4},{6,7},{9,8},{10,11},{13,12},{14,15},{17,16},{18,... | collective-permute-start | bytes 3145736 | tf_op jit(solution)/shard_map/ppermute | solution.py:1202
  285.9 22.6 %collective-permute-start.38 = (bf16[2,192,1024]{2,1,0:T(8,128)(2,1)S(1)}, bf16[2,192,1024]{2,1,0:T(8,128)(2,1)S(1)}, u32[]{:S(2)}, u32[]{:S(2)}) collective-permute-start(bf16[2,192,1024]{2,1,0:T(8,128)(2,1)S(1)} %get-tuple-element.344), channel_id=1, source_target_pairs={{0,16},{4,20},{8,24},{12,28},{16,0},{20,4},{24,8},{28,12},{1,17},{... | collective-permute-start | bytes 2359304 | tf_op jit(solution)/shard_map/ppermute | solution.py:35
  288.2 22.3 %collective-permute-start.37 = (bf16[2,192,1024]{2,1,0:T(8,128)(2,1)S(1)}, bf16[2,192,1024]{2,1,0:T(8,128)(2,1)S(1)}, u32[]{:S(2)}, u32[]{:S(2)}) collective-permute-start(bf16[2,192,1024]{2,1,0:T(8,128)(2,1)S(1)} %get-tuple-element.341), channel_id=1, source_target_pairs={{0,8},{4,12},{8,0},{12,4},{16,24},{20,28},{24,16},{28,20},{1,9},{5... | collective-permute-start | bytes 2359304 | tf_op jit(solution)/shard_map/ppermute | solution.py:35
  300.5 20.4 %collective-permute-start.40 = (bf16[256,1024]{1,0:T(8,128)(2,1)}, bf16[256,1024]{1,0:T(8,128)(2,1)S(1)}, u32[]{:S(2)}, u32[]{:S(2)}) collective-permute-start(bf16[256,1024]{1,0:T(8,128)(2,1)} %get-tuple-element.349), channel_id=1, source_target_pairs={{0,8},{4,12},{8,0},{12,4},{16,24},{20,28},{24,16},{28,20},{1,9},{5... | collective-permute-start | bytes 1572872 | tf_op jit(solution)/shard_map/ppermute | solution.py:35
  301.8 20.0 %collective-permute-start.39 = (bf16[256,1024]{1,0:T(8,128)(2,1)}, bf16[256,1024]{1,0:T(8,128)(2,1)S(1)}, u32[]{:S(2)}, u32[]{:S(2)}) collective-permute-start(bf16[256,1024]{1,0:T(8,128)(2,1)} %get-tuple-element.347), channel_id=1, source_target_pairs={{0,16},{4,20},{8,24},{12,28},{16,0},{20,4},{24,8},{28,12},{1,17},{... | collective-permute-start | bytes 1572872 | tf_op jit(solution)/shard_map/ppermute | solution.py:35
  329.0 37.8 %collective-permute-start.55 = (bf16[512,1024]{1,0:T(8,128)(2,1)S(1)}, bf16[512,1024]{1,0:T(8,128)(2,1)S(1)}, u32[]{:S(2)}, u32[]{:S(2)}) collective-permute-start(bf16[512,1024]{1,0:T(8,128)(2,1)S(1)} %copy-done.103), channel_id=1, source_target_pairs={{1,0},{2,3},{5,4},{6,7},{9,8},{10,11},{13,12},{14,15},{17,16},{18,... | collective-permute-start | bytes 3145736 | tf_op jit(solution)/shard_map/ppermute | solution.py:1202
  330.3 20.3 %collective-permute-start.42 = (bf16[192,1024]{1,0:T(8,128)(2,1)S(1)}, bf16[192,1024]{1,0:T(8,128)(2,1)S(1)}, u32[]{:S(2)}, u32[]{:S(2)}) collective-permute-start(bf16[192,1024]{1,0:T(8,128)(2,1)S(1)} %copy-done.95), channel_id=1, source_target_pairs={{0,8},{4,12},{8,0},{12,4},{16,24},{20,28},{24,16},{28,20},{1,9},{5... | collective-permute-start | bytes 1179656 | tf_op jit(solution)/shard_map/ppermute | solution.py:35
  331.6 18.9 %collective-permute-start.41 = (bf16[192,1024]{1,0:T(8,128)(2,1)S(1)}, bf16[192,1024]{1,0:T(8,128)(2,1)S(1)}, u32[]{:S(2)}, u32[]{:S(2)}) collective-permute-start(bf16[192,1024]{1,0:T(8,128)(2,1)S(1)} %get-tuple-element.351), channel_id=1, source_target_pairs={{0,16},{4,20},{8,24},{12,28},{16,0},{20,4},{24,8},{28,12},{1,17},{... | collective-permute-start | bytes 1179656 | tf_op jit(solution)/shard_map/ppermute | solution.py:35
  332.0 21.9 %collective-permute-start.46 = (bf16[256,1024]{1,0:T(8,128)(2,1)S(1)}, bf16[256,1024]{1,0:T(8,128)(2,1)S(1)}, u32[]{:S(2)}, u32[]{:S(2)}) collective-permute-start(bf16[256,1024]{1,0:T(8,128)(2,1)S(1)} %get-tuple-element.359), channel_id=1, source_target_pairs={{0,1},{3,2},{4,5},{7,6},{8,9},{11,10},{12,13},{15,14},{16,17},{19,... | collective-permute-start | bytes 1572872 | tf_op jit(solution)/shard_map/ppermute | solution.py:1202
  345.5 19.7 %collective-permute-start.47 = (bf16[256,1024]{1,0:T(8,128)(2,1)S(1)}, bf16[256,1024]{1,0:T(8,128)(2,1)S(1)}, u32[]{:S(2)}, u32[]{:S(2)}) collective-permute-start(bf16[256,1024]{1,0:T(8,128)(2,1)S(1)} %get-tuple-element.362), channel_id=1, source_target_pairs={{0,1},{3,2},{4,5},{7,6},{8,9},{11,10},{12,13},{15,14},{16,17},{19,... | collective-permute-start | bytes 1572872 | tf_op jit(solution)/shard_map/ppermute | solution.py:1202
  351.5 27.8 %collective-permute-start.48 = (bf16[392,1024]{1,0:T(8,128)(2,1)S(1)}, bf16[392,1024]{1,0:T(8,128)(2,1)S(1)}, u32[]{:S(2)}, u32[]{:S(2)}) collective-permute-start(bf16[392,1024]{1,0:T(8,128)(2,1)S(1)} %pad_maximum_fusion.2), channel_id=1, source_target_pairs={{0,1},{3,2},{4,5},{7,6},{8,9},{11,10},{12,13},{15,14},{16,17},{19,... | collective-permute-start | bytes 2408456 | tf_op jit(solution)/shard_map/ppermute | solution.py:1202
  365.4 15.2 %collective-permute-start.49 = (bf16[256,1024]{1,0:T(8,128)(2,1)S(1)}, bf16[256,1024]{1,0:T(8,128)(2,1)S(1)}, u32[]{:S(2)}, u32[]{:S(2)}) collective-permute-start(bf16[256,1024]{1,0:T(8,128)(2,1)S(1)} %add_convert_fusion.9), channel_id=1, source_target_pairs={{1,2},{2,1},{5,6},{6,5},{9,10},{10,9},{13,14},{14,13},{17,18},{18,... | collective-permute-start | bytes 1572872 | tf_op jit(solution)/shard_map/ppermute | solution.py:1202
  366.1 14.7 %collective-permute-start.50 = (bf16[256,1024]{1,0:T(8,128)(2,1)S(1)}, bf16[256,1024]{1,0:T(8,128)(2,1)S(1)}, u32[]{:S(2)}, u32[]{:S(2)}) collective-permute-start(bf16[256,1024]{1,0:T(8,128)(2,1)S(1)} %add_convert_fusion.8), channel_id=1, source_target_pairs={{1,2},{2,1},{5,6},{6,5},{9,10},{10,9},{13,14},{14,13},{17,18},{18,... | collective-permute-start | bytes 1572872 | tf_op jit(solution)/shard_map/ppermute | solution.py:1202
  381.0 21.6 %collective-permute-start.53 = (bf16[256,1024]{1,0:T(8,128)(2,1)S(1)}, bf16[256,1024]{1,0:T(8,128)(2,1)S(1)}, u32[]{:S(2)}, u32[]{:S(2)}) collective-permute-start(bf16[256,1024]{1,0:T(8,128)(2,1)S(1)} %add_convert_fusion.6), channel_id=1, source_target_pairs={{1,0},{2,3},{5,4},{6,7},{9,8},{10,11},{13,12},{14,15},{17,16},{18,... | collective-permute-start | bytes 1572872 | tf_op jit(solution)/shard_map/ppermute | solution.py:1202
  382.4 30.2 %collective-permute-start.54 = (bf16[256,1024]{1,0:T(8,128)(2,1)S(1)}, bf16[256,1024]{1,0:T(8,128)(2,1)S(1)}, u32[]{:S(2)}, u32[]{:S(2)}) collective-permute-start(bf16[256,1024]{1,0:T(8,128)(2,1)S(1)} %add_convert_fusion.7), channel_id=1, source_target_pairs={{1,0},{2,3},{5,4},{6,7},{9,8},{10,11},{13,12},{14,15},{17,16},{18,... | collective-permute-start | bytes 1572872 | tf_op jit(solution)/shard_map/ppermute | solution.py:1202
  385.5 39.9 %collective-permute-start.52 = (bf16[392,1024]{1,0:T(8,128)(2,1)S(1)}, bf16[392,1024]{1,0:T(8,128)(2,1)S(1)}, u32[]{:S(2)}, u32[]{:S(2)}) collective-permute-start(bf16[392,1024]{1,0:T(8,128)(2,1)S(1)} %add_convert_fusion.4), channel_id=1, source_target_pairs={{1,0},{2,3},{5,4},{6,7},{9,8},{10,11},{13,12},{14,15},{17,16},{18,... | collective-permute-start | bytes 2408456 | tf_op jit(solution)/shard_map/ppermute | solution.py:1202
  (134 other events, 1640.5 us)
where the time goes:
time: 436 us; the launch traced here: 428 us
  Pallas kernels  190 us (44%)
  waiting for transfers between devices  110 us (25%)
  starting transfers between devices  73.6 us (17%)
  local copies, waits for them, and re-layouts  36.4 us (8%)
  other arithmetic  15 us (3%)
    pallas_call x35, Pallas kernels, run(): pl.pallas_call(kernel, out_shape=outs, grid_spec=pltpu.PrefetchScalarGrid...  190 us
    ppermute x15, waiting for transfers between devices, send(): self.recv = lax.ppermute(clock.at(self.value), 'dp', self.rounds[0][0])  59 us
    ppermute x39, waiting for transfers between devices, swapped(): lax.ppermute(value, axis, [(place, place ^ distance) for place in range(c...  51.2 us
    ppermute x39, starting transfers between devices, swapped(): lax.ppermute(value, axis, [(place, place ^ distance) for place in range(c...  37.8 us
    ppermute x15, starting transfers between devices, send(): self.recv = lax.ppermute(clock.at(self.value), 'dp', self.rounds[0][0])  32.1 us
    unnamed x233, local copies, waits for them, and re-layouts  30.8 us
    convert_element_type x13, other arithmetic, add_low(): return total.astype(BF)  9.1 us
  transfers between devices with their start and end apart: 56, of which 27 were waited for; matrix products, arithmetic and copies ran while one was open for 4% of the time, Pallas kernels for 32%

commit v1 on v0

--- a/solution.py
+++ b/solution.py
@@ -1172,6 +1172,7 @@
         args += more[0]
         specs += more[1]
     total = sum(arg.shape[0] for arg in args[2::3])
+    args = [pltpu.with_memory_space_constraint(arg, pltpu.HBM) for arg in args]
     return clock.run(
         pack_kernel,
         (shape((total, D), BF),),

time: 436 us -> 434 us (level)
    unnamed x233 -> x215, local copies, waits for them, and re-layouts: 30.8 us -> 27.8 us
  transfers between devices with their start and end apart: 56 -> 56, of which waited for: 27 -> 26; matrix products, arithmetic and copies ran while one was open for 4% -> 4% of each run, Pallas kernels for 32% -> 33%
where the time goes in v1:
time: 434 us; the launch traced here: 425 us
  Pallas kernels  192 us (44%)
  waiting for transfers between devices  110 us (25%)
  starting transfers between devices  74 us (17%)
  local copies, waits for them, and re-layouts  32.1 us (7%)
  other arithmetic  13.9 us (3%)
    pallas_call x35, Pallas kernels, run(): pl.pallas_call(kernel, out_shape=outs, grid_spec=pltpu.PrefetchScalarGrid...  192 us
    ppermute x15, waiting for transfers between devices, send(): self.recv = lax.ppermute(clock.at(self.value), 'dp', self.rounds[0][0])  56.2 us
    ppermute x39, waiting for transfers between devices, swapped(): lax.ppermute(value, axis, [(place, place ^ distance) for place in range(c...  53.6 us
    ppermute x39, starting transfers between devices, swapped(): lax.ppermute(value, axis, [(place, place ^ distance) for place in range(c...  38 us
    ppermute x15, starting transfers between devices, send(): self.recv = lax.ppermute(clock.at(self.value), 'dp', self.rounds[0][0])  32.3 us
    unnamed x215, local copies, waits for them, and re-layouts  27.8 us
  transfers between devices with their start and end apart: 56, of which 26 were waited for; matrix products, arithmetic and copies ran while one was open for 4% of the time, Pallas kernels for 33%

profile of v1, /device:TPU:0, one launch (start us, length us, event | category | flops | bytes accessed | tf_op | source)
XLA Modules:
  0.0 425.2 jit_solution(16802490410520409250)
XLA Ops:
  5.7 7.3 %shard_map.271 = (bf16[512,1024]{1,0:T(8,128)(2,1)S(1)}, bf16[512,1024]{1,0:T(8,128)(2,1)S(1)}, bf16[2,512,1024]{2,1,0:T(8,128)(2,1)S(1)}) custom-call(s32[3]{0:T(128)S(1)} %pad_add_fusion.flags, bf16[512,1024]{1,0:T(8,128)(2,1)S(1)} %bitcast.72, f32[1,1024]{1,0:T(1,128)S(1)} %bitcast.80, bf16[1024,1024]{1,0:T(8,128)(2,1)} %wq.3, bf16[1024,1024]{1,0:T(8,128)(2,1)} %wk.9, ...), custom_call_target="tpu_custom_call" | custom-call | flops 3221225472 | bytes 11538432 | tf_op jit(solution)/shard_map/pallas_call | solution.py:103
  14.1 10.9 %shard_map.272 = (bf16[512,1024]{1,0:T(8,128)(2,1)S(1)}, f32[512,1024]{1,0:T(8,128)S(1)}, f32[512,1024]{1,0:T(8,128)S(1)}, bf16[2,256,1024]{2,1,0:T(8,128)(2,1)S(1)}, bf16[2,256,1024]{2,1,0:T(8,128)(2,1)S(1)}) custom-call(s32[3]{0:T(128)S(1)} %pad_add_fusion.flags, bf16[512,1024]{1,0:T(8,128)(2,1)S(1)} %copy-done.65, ...), custom_call_target="tpu_custom_call" | custom-call | flops 3221225472 | bytes 20975616 | tf_op jit(solution)/shard_map/pallas_call | solution.py:103
  27.6 4.6 %shard_map.273.refs_1_.left = bf16[2,512,1024]{2,1,0:T(8,128)(2,1)S(1)} custom-call(s32[3]{0:T(128)S(1)} %pad_add_fusion.flags, bf16[512,1024]{1,0:T(8,128)(2,1)S(1)} %collective-permute-done.tokens, f32[1,1024]{1,0:T(1,128)S(1)} %bitcast.81, bf16[1024,1024]{1,0:T(8,128)(2,1)S(1)} %copy-done.8, bf16[1024,1024]{1,0:T(8,128)(2,1)S(1)} %copy-done.11), custom_call_target="tpu_custom_call" | custom-call | flops 99999997952 | bytes 7344128 | tf_op jit(solution)/shard_map/pallas_call | solution.py:103
  38.6 6.6 %shard_map.275 = (bf16[512,2048]{1,0:T(8,128)(2,1)S(1)}, bf16[512,2048]{1,0:T(8,128)(2,1)S(1)}) custom-call(s32[3]{0:T(128)S(1)} %pad_add_fusion.flags, bf16[512,1024]{1,0:T(8,128)(2,1)S(1)} %bitcast.61, bf16[8,512,1024]{2,1,0:T(8,128)(2,1)S(1)} %bitcast.59, bf16[8,512,1024]{2,1,0:T(8,128)(2,1)S(1)} %bitcast.60), custom_call_target="tpu_custom_call" | custom-call | flops 4294967296 | bytes 22020096 | tf_op jit(solution)/shard_map/pallas_call | solution.py:103
  45.2 5.0 %collective-permute-done.3.from2.kept2 = bf16[2,64,1024]{2,1,0:T(8,128)(2,1)S(1)} collective-permute-done((bf16[2,64,1024]{2,1,0:T(8,128)(2,1)S(1)}, bf16[2,64,1024]{2,1,0:T(8,128)(2,1)S(1)}, u32[]{:S(2)}, u32[]{:S(2)}) %collective-permute-start.3) | collective-permute-done | bytes 262176 | tf_op jit(solution)/shard_map/ppermute | solution.py:35
  62.7 5.5 %shard_map.278 = (f32[512,1024]{1,0:T(8,128)S(1)}, bf16[512,1024]{1,0:T(8,128)(2,1)S(1)}, f32[512,1024]{1,0:T(8,128)}, bf16[2,512,1024]{2,1,0:T(8,128)(2,1)S(1)}) custom-call(s32[3]{0:T(128)S(1)} %pad_add_fusion.flags, bf16[256,1024]{1,0:T(8,128)(2,1)S(1)} %get-tuple-element.219.mine, bf16[256,1024]{1,0:T(8,128)(2,1)S(1)} %collective-permute-done.8.other, ...), custom_call_target="tpu_custom_call" | custom-call | flops 2147483648 | bytes 18874368 | tf_op jit(solution)/shard_map/pallas_call | solution.py:103
  69.5 14.3 %shard_map.279 = (bf16[512,1024]{1,0:T(8,128)(2,1)S(1)}, f32[8,1,512]{2,1,0:T(1,128)S(1)}) custom-call(s32[3]{0:T(128)S(1)} %pad_add_fusion.flags, bf16[512,1024]{1,0:T(8,128)(2,1)} %copy-done.85, bf16[2,512,1024]{2,1,0:T(8,128)(2,1)} %copy-done.84, bf16[2,512,1024]{2,1,0:T(8,128)(2,1)} %copy-done.53, bf16[2,512,1024]{2,1,0:T(8,128)(2,1)} %copy-done.80), custom_call_target="tpu_custom_call" | custom-call | flops 3221225472 | bytes 8404992 | tf_op jit(solution)/shard_map/pallas_call | solution.py:103
  83.8 13.4 %shard_map.280 = (bf16[512,2048]{1,0:T(8,128)(2,1)S(1)}, bf16[512,2048]{1,0:T(8,128)(2,1)S(1)}, bf16[512,1024]{1,0:T(8,128)(2,1)S(1)}, f32[512,1024]{1,0:T(8,128...) custom-call(s32[3]{0:T(128)S(1)} %pad_add_fusion.flags, ...), custom_call_target="tpu_custom_call" | custom-call | flops 7516192768 | bytes 42995712 | tf_op jit(solution)/shard_map/pallas_call | solution.py:103
  100.0 3.6 shard_map.281
  103.7 7.0 %collective-permute-done.9.refs_4_ = bf16[4,512,1024]{2,1,0:T(8,128)(2,1)S(1)} collective-permute-done((bf16[4,512,1024]{2,1,0:T(8,128)(2,1)S(1)}, bf16[4,512,1024]{2,1,0:T(8,128)(2,1)S(1)}, u32[]{:S(2)}, u32[]{:S(2)}) %collective-permute-start.9) | collective-permute-done | bytes 4194336 | tf_op jit(solution)/shard_map/ppermute | solution.py:35
  110.8 4.5 %shard_map.282 = (bf16[2,256,1024]{2,1,0:T(8,128)(2,1)S(1)}, bf16[2,256,1024]{2,1,0:T(8,128)(2,1)S(1)}, bf16[2,256,1024]{2,1,0:T(8,128)(2,1)}, bf16[2,256,1024]{2,1,0:T(8,128)(2,1)S(1)}) custom-call(s32[3]{0:T(128)S(1)} %pad_add_fusion.flags, bf16[512,2048]{1,0:T(8,128)(2,1)S(1)} %get-tuple-element.230.refs_0_, ...), custom_call_target="tpu_custom_call" | custom-call | flops 2147483648 | bytes 14680064 | tf_op jit(solution)/shard_map/pallas_call | solution.py:103
  120.5 15.9 %shard_map.283 = (bf16[512,2048]{1,0:T(8,128)(2,1)S(1)}, bf16[512,2048]{1,0:T(8,128)(2,1)S(1)}, bf16[512,1024]{1,0:T(8,128)(2,1)}, f32[512,1024]{1,0:T(8,128)S(1...) custom-call(s32[3]{0:T(128)S(1)} %pad_add_fusion.flags, ...), custom_call_target="tpu_custom_call" | custom-call | flops 7516192768 | bytes 47194112 | tf_op jit(solution)/shard_map/pallas_call | solution.py:103
  136.4 3.6 shard_map.284
  147.2 4.6 %shard_map.286 = (bf16[2,256,1024]{2,1,0:T(8,128)(2,1)S(1)}, bf16[2,256,1024]{2,1,0:T(8,128)(2,1)S(1)}, bf16[2,256,1024]{2,1,0:T(8,128)(2,1)}, bf16[2,256,1024]{2,1,0:T(8,128)(2,1)S(1)}) custom-call(s32[3]{0:T(128)S(1)} %pad_add_fusion.flags, bf16[512,2048]{1,0:T(8,128)(2,1)S(1)} %get-tuple-element.244.refs_0_, ...), custom_call_target="tpu_custom_call" | custom-call | flops 2147483648 | bytes 14680064 | tf_op jit(solution)/shard_map/pallas_call | solution.py:103
  153.8 23.0 %shard_map.287 = (bf16[512,1024]{1,0:T(8,128)(2,1)S(1)}, bf16[2,512,1024]{2,1,0:T(8,128)(2,1)S(1)}, f32[2,512,1024]{2,1,0:T(8,128)S(1)}, bf16[2,512,1024]{2,1,0:T(8,128)(2,1)S(1)}) custom-call(s32[3]{0:T(128)S(1)} %pad_add_fusion.flags, bf16[512,1024]{1,0:T(8,128)(2,1)} %copy-done.85, bf16[2,512,1024]{2,1,0:T(8,128)(2,1)} %copy-done.84, ...), custom_call_target="tpu_custom_call" | custom-call | flops 8053063680 | bytes 17842176 | tf_op jit(solution)/shard_map/pallas_call | solution.py:103
  176.9 4.3 %shard_map.288 = (f32[512,1024]{1,0:T(8,128)S(1)}, bf16[256,1024]{1,0:T(8,128)(2,1)S(1)}, bf16[256,1024]{1,0:T(8,128)(2,1)S(1)}) custom-call(s32[3]{0:T(128)S(1)} %pad_add_fusion.flags, bf16[2,512,1024]{2,1,0:T(8,128)(2,1)S(1)} %get-tuple-element.262.state_grad.refs_4_.refs_7_, bf16[1024,1024]{1,0:T(8,128)(2,1)S(1)} %copy-done.9, ...), custom_call_target="tpu_custom_call" | custom-call | flops 2147483648 | bytes 13631488 | tf_op jit(solution)/shard_map/pallas_call | solution.py:103
  213.4 6.9 %shard_map.294 = (bf16[512,1024]{1,0:T(8,128)(2,1)S(1)}, bf16[2,512,1024]{2,1,0:T(8,128)(2,1)S(1)}, f32[1,1024]{1,0:T(1,128)S(1)}, bf16[512,1024]{1,0:T(8,128)(2,1)S(1)}) custom-call(s32[3]{0:T(128)S(1)} %pad_add_fusion.flags, bf16[256,1024]{1,0:T(8,128)(2,1)S(1)} %get-tuple-element.288.mine, bf16[256,1024]{1,0:T(8,128)(2,1)S(1)} %collective-permute-done.25.other, ...), custom_call_target="tpu_custom_call" | custom-call | flops 2147483648 | bytes 24121344 | tf_op jit(solution)/shard_map/pallas_call | solution.py:103
  220.3 3.7 shard_map.295
  232.9 12.3 %shard_map.297 = (bf16[512,1024]{1,0:T(8,128)(2,1)S(1)}, bf16[2,512,1024]{2,1,0:T(8,128)(2,1)S(1)}) custom-call(s32[3]{0:T(128)S(1)} %pad_add_fusion.flags, bf16[512,1024]{1,0:T(8,128)(2,1)} %refs_0_.1, bf16[2,512,1024]{2,1,0:T(8,128)(2,1)} %copy-done.53, bf16[512,1024]{1,0:T(8,128)(2,1)} %copy-done.82, f32[2,512,1024]{2,1,0:T(8,128)} %copy-done.83), custom_call_target="tpu_custom_call" | custom-call | flops 2684354560 | bytes 11534336 | tf_op jit(solution)/shard_map/pallas_call | solution.py:103
  249.8 5.0 %shard_map.298 = (bf16[2,256,1024]{2,1,0:T(8,128)(2,1)}, bf16[2,256,1024]{2,1,0:T(8,128)(2,1)S(1)}, bf16[2,256,1024]{2,1,0:T(8,128)(2,1)}, bf16[2,256,1024]{2,1,0:T(8,128)(2,1)S(1)}) custom-call(s32[3]{0:T(128)S(1)} %pad_add_fusion.flags, bf16[512,1024]{1,0:T(8,128)(2,1)S(1)} %get-tuple-element.228.attended.refs_0_, bf16[512,1024]{1,0:T(8,128)(2,1)S(1)} %copy-done.47, ...), custom_call_target="tpu_custom_call" | custom-call | flops 2147483648 | bytes 17825792 | tf_op jit(solution)/shard_map/pallas_call | solution.py:103
  258.1 5.0 %shard_map.299 = bf16[4,384,1024]{2,1,0:T(8,128)(2,1)} custom-call(s32[3]{0:T(128)S(1)} %pad_add_fusion.flags, bf16[512,1024]{1,0:T(8,128)(2,1)S(1)} %get-tuple-element.199.refs_2_.refs_0_, bf16[512,1024]{1,0:T(8,128)(2,1)S(1)} %get-tuple-element.316.refs_1_, bf16[2,512,1024]{2,1,0:T(8,128)(2,1)S(1)} %get-tuple-element.317.refs_2_.refs_5_.pair_total, ...), custom_call_target="tpu_custom_call" | custom-call | flops 3221225472 | bytes 19922944 | tf_op jit(solution)/shard_map/pallas_call | solution.py:103
  276.8 6.0 %shard_map.300 = (bf16[2,192,1024]{2,1,0:T(8,128)(2,1)S(1)}, bf16[2,192,1024]{2,1,0:T(8,128)(2,1)S(1)}, bf16[2,192,1024]{2,1,0:T(8,128)(2,1)S(1)}, bf16[2,192,1024]{2,1,0:T(8,128)(2,1)S(1)}) custom-call(s32[3]{0:T(128)S(1)} %pad_add_fusion.flags, bf16[512,1024]{1,0:T(8,128)(2,1)S(1)} %get-tuple-element.199.refs_2_.refs_0_, bf16[512,1024]{1,0:T(8,128)(2,1)S(1)} %copy-done.31, ...), custom_call_target="tpu_custom_call" | custom-call | flops 3221225472 | bytes 23068672 | tf_op jit(solution)/shard_map/pallas_call | solution.py:103
  289.5 8.7 %shard_map.301 = (f32[512,1024]{1,0:T(8,128)}, f32[1,1024]{1,0:T(1,128)S(1)}) custom-call(s32[3]{0:T(128)S(1)} %pad_add_fusion.flags, bf16[512,1024]{1,0:T(8,128)(2,1)S(1)} %copy-done.21, bf16[2,512,1024]{2,1,0:T(8,128)(2,1)S(1)} %copy-done.4, bf16[2,512,1024]{2,1,0:T(8,128)(2,1)S(1)} %collective-permute-done.31.refs_3_.refs_6_.returned, ...), custom_call_target="tpu_custom_call" | custom-call | flops 3221225472 | bytes 16785408 | tf_op jit(solution)/shard_map/pallas_call | solution.py:103
  304.3 4.7 %collective-permute-done.38.recv2.refs_4_ = bf16[2,192,1024]{2,1,0:T(8,128)(2,1)S(1)} collective-permute-done((bf16[2,192,1024]{2,1,0:T(8,128)(2,1)S(1)}, bf16[2,192,1024]{2,1,0:T(8,128)(2,1)S(1)}, u32[]{:S(2)}, u32[]{:S(2)}) %collective-permute-start.38) | collective-permute-done | bytes 786464 | tf_op jit(solution)/shard_map/ppermute | solution.py:35
  312.0 9.5 %collective-permute-done.40.refs_5_ = bf16[256,1024]{1,0:T(8,128)(2,1)S(1)} collective-permute-done((bf16[256,1024]{1,0:T(8,128)(2,1)S(1)}, bf16[256,1024]{1,0:T(8,128)(2,1)S(1)}, u32[]{:S(2)}, u32[]{:S(2)}) %collective-permute-start.40) | collective-permute-done | bytes 524320 | tf_op jit(solution)/shard_map/ppermute | solution.py:35
  328.9 9.6 %collective-permute-start.46 = (bf16[256,1024]{1,0:T(8,128)(2,1)S(1)}, bf16[256,1024]{1,0:T(8,128)(2,1)S(1)}, u32[]{:S(2)}, u32[]{:S(2)}) collective-permute-start(bf16[256,1024]{1,0:T(8,128)(2,1)S(1)} %get-tuple-element.359), channel_id=1, source_target_pairs={{0,1},{3,2},{4,5},{7,6},{8,9},{11,10},{12,13},{15,14},{16,17},{19,... | collective-permute-start | bytes 1572872 | tf_op jit(solution)/shard_map/ppermute | solution.py:1203
  342.4 5.3 %collective-permute-start.47 = (bf16[256,1024]{1,0:T(8,128)(2,1)S(1)}, bf16[256,1024]{1,0:T(8,128)(2,1)S(1)}, u32[]{:S(2)}, u32[]{:S(2)}) collective-permute-start(bf16[256,1024]{1,0:T(8,128)(2,1)S(1)} %get-tuple-element.362), channel_id=1, source_target_pairs={{0,1},{3,2},{4,5},{7,6},{8,9},{11,10},{12,13},{15,14},{16,17},{19,... | collective-permute-start | bytes 1572872 | tf_op jit(solution)/shard_map/ppermute | solution.py:1203
  353.2 8.8 %collective-permute-done.47 = bf16[256,1024]{1,0:T(8,128)(2,1)S(1)} collective-permute-done((bf16[256,1024]{1,0:T(8,128)(2,1)S(1)}, bf16[256,1024]{1,0:T(8,128)(2,1)S(1)}, u32[]{:S(2)}, u32[]{:S(2)}) %collective-permute-start.47) | collective-permute-done | bytes 524320 | tf_op jit(solution)/shard_map/ppermute | solution.py:1203
  365.2 11.2 %collective-permute-done.48 = bf16[392,1024]{1,0:T(8,128)(2,1)S(1)} collective-permute-done((bf16[392,1024]{1,0:T(8,128)(2,1)S(1)}, bf16[392,1024]{1,0:T(8,128)(2,1)S(1)}, u32[]{:S(2)}, u32[]{:S(2)}) %collective-permute-start.48) | collective-permute-done | bytes 802848 | tf_op jit(solution)/shard_map/ppermute | solution.py:1203
  383.8 15.9 %collective-permute-done.53 = bf16[256,1024]{1,0:T(8,128)(2,1)S(1)} collective-permute-done((bf16[256,1024]{1,0:T(8,128)(2,1)S(1)}, bf16[256,1024]{1,0:T(8,128)(2,1)S(1)}, u32[]{:S(2)}, u32[]{:S(2)}) %collective-permute-start.53) | collective-permute-done | bytes 524320 | tf_op jit(solution)/shard_map/ppermute | solution.py:1203
  399.7 10.1 %collective-permute-done.54 = bf16[256,1024]{1,0:T(8,128)(2,1)S(1)} collective-permute-done((bf16[256,1024]{1,0:T(8,128)(2,1)S(1)}, bf16[256,1024]{1,0:T(8,128)(2,1)S(1)}, u32[]{:S(2)}, u32[]{:S(2)}) %collective-permute-start.54) | collective-permute-done | bytes 524320 | tf_op jit(solution)/shard_map/ppermute | solution.py:1203
  412.7 9.8 %collective-permute-done.52 = bf16[392,1024]{1,0:T(8,128)(2,1)S(1)} collective-permute-done((bf16[392,1024]{1,0:T(8,128)(2,1)S(1)}, bf16[392,1024]{1,0:T(8,128)(2,1)S(1)}, u32[]{:S(2)}, u32[]{:S(2)}) %collective-permute-start.52) | collective-permute-done | bytes 802848 | tf_op jit(solution)/shard_map/ppermute | solution.py:1203
  (372 shorter events, 156.0 us)
Async XLA Ops:
  0.6 27.0 %collective-permute-start = (bf16[512,1024]{1,0:T(8,128)(2,1)}, bf16[512,1024]{1,0:T(8,128)(2,1)S(1)}, u32[]{:S(2)}, u32[]{:S(2)}) collective-permute-start(bf16[512,1024]{1,0:T(8,128)(2,1)} %bitcast.71), channel_id=1, source_target_pairs={{0,4},{4,8},{8,12},{12,16},{16,20},{20,24},{24,28},{1,5},{5,9},{9,... | collective-permute-start | bytes 3145736 | tf_op jit(solution)/shard_map/ppermute | solution.py:41
  115.3 25.4 %collective-permute-start.11 = (bf16[2,256,1024]{2,1,0:T(8,128)(2,1)}, bf16[2,256,1024]{2,1,0:T(8,128)(2,1)S(1)}, u32[]{:S(2)}, u32[]{:S(2)}) collective-permute-start(bf16[2,256,1024]{2,1,0:T(8,128)(2,1)} %get-tuple-element.252), channel_id=1, source_target_pairs={{0,16},{4,20},{8,24},{12,28},{16,0},{20,4},{24,8},{28,12},{1,17},{... | collective-permute-start | bytes 3145736 | tf_op jit(solution)/shard_map/ppermute | solution.py:35
  116.3 24.9 %collective-permute-start.10 = (bf16[2,256,1024]{2,1,0:T(8,128)(2,1)S(1)}, bf16[2,256,1024]{2,1,0:T(8,128)(2,1)S(1)}, u32[]{:S(2)}, u32[]{:S(2)}) collective-permute-start(bf16[2,256,1024]{2,1,0:T(8,128)(2,1)S(1)} %get-tuple-element.249), channel_id=1, source_target_pairs={{0,8},{4,12},{8,0},{12,4},{16,24},{20,28},{24,16},{28,20},{1,9},{5... | collective-permute-start | bytes 3145736 | tf_op jit(solution)/shard_map/ppermute | solution.py:35
  143.0 38.3 %collective-permute-start.14 = (bf16[256,1024]{1,0:T(8,128)(2,1)}, bf16[256,1024]{1,0:T(8,128)(2,1)}, u32[]{:S(2)}, u32[]{:S(2)}) collective-permute-start(bf16[256,1024]{1,0:T(8,128)(2,1)} %get-tuple-element.267), channel_id=1, source_target_pairs={{0,8},{4,12},{8,0},{12,4},{16,24},{20,28},{24,16},{28,20},{1,9},{5... | collective-permute-start | bytes 1572872 | tf_op jit(solution)/shard_map/ppermute | solution.py:35
  143.9 37.3 %collective-permute-start.13 = (bf16[256,1024]{1,0:T(8,128)(2,1)}, bf16[256,1024]{1,0:T(8,128)(2,1)}, u32[]{:S(2)}, u32[]{:S(2)}) collective-permute-start(bf16[256,1024]{1,0:T(8,128)(2,1)} %get-tuple-element.265), channel_id=1, source_target_pairs={{0,16},{4,20},{8,24},{12,28},{16,0},{20,4},{24,8},{28,12},{1,17},{... | collective-permute-start | bytes 1572872 | tf_op jit(solution)/shard_map/ppermute | solution.py:35
  151.7 41.2 %collective-permute-start.17 = (bf16[2,256,1024]{2,1,0:T(8,128)(2,1)}, bf16[2,256,1024]{2,1,0:T(8,128)(2,1)S(1)}, u32[]{:S(2)}, u32[]{:S(2)}) collective-permute-start(bf16[2,256,1024]{2,1,0:T(8,128)(2,1)} %get-tuple-element.277), channel_id=1, source_target_pairs={{0,16},{4,20},{8,24},{12,28},{16,0},{20,4},{24,8},{28,12},{1,17},{... | collective-permute-start | bytes 3145736 | tf_op jit(solution)/shard_map/ppermute | solution.py:35
  152.5 41.8 %collective-permute-start.16 = (bf16[2,256,1024]{2,1,0:T(8,128)(2,1)S(1)}, bf16[2,256,1024]{2,1,0:T(8,128)(2,1)S(1)}, u32[]{:S(2)}, u32[]{:S(2)}) collective-permute-start(bf16[2,256,1024]{2,1,0:T(8,128)(2,1)S(1)} %get-tuple-element.274), channel_id=1, source_target_pairs={{0,8},{4,12},{8,0},{12,4},{16,24},{20,28},{24,16},{28,20},{1,9},{5... | collective-permute-start | bytes 3145736 | tf_op jit(solution)/shard_map/ppermute | solution.py:35
  184.1 28.8 %collective-permute-start.24 = (bf16[512,1024]{1,0:T(8,128)(2,1)S(1)}, bf16[512,1024]{1,0:T(8,128)(2,1)S(1)}, u32[]{:S(2)}, u32[]{:S(2)}) collective-permute-start(bf16[512,1024]{1,0:T(8,128)(2,1)S(1)} %shard_map.289), channel_id=1, source_target_pairs={{0,1},{3,2},{4,5},{7,6},{8,9},{11,10},{12,13},{15,14},{16,17},{19,... | collective-permute-start | bytes 3145736 | tf_op jit(solution)/shard_map/ppermute | solution.py:1203
  210.7 14.3 %collective-permute-start.27 = (bf16[256,1024]{1,0:T(8,128)(2,1)S(1)}, bf16[256,1024]{1,0:T(8,128)(2,1)S(1)}, u32[]{:S(2)}, u32[]{:S(2)}) collective-permute-start(bf16[256,1024]{1,0:T(8,128)(2,1)S(1)} %get-tuple-element.301), channel_id=1, source_target_pairs={{0,8},{4,12},{8,0},{12,4},{16,24},{20,28},{24,16},{28,20},{1,9},{5... | collective-permute-start | bytes 1572872 | tf_op jit(solution)/shard_map/ppermute | solution.py:35
  229.4 15.8 %collective-permute-start.28 = (bf16[4,512,1024]{2,1,0:T(8,128)(2,1)S(1)}, bf16[4,512,1024]{2,1,0:T(8,128)(2,1)S(1)}, u32[]{:S(2)}, u32[]{:S(2)}) collective-permute-start(bf16[4,512,1024]{2,1,0:T(8,128)(2,1)S(1)} %shard_map.295), channel_id=1, source_target_pairs={{0,4},{4,0},{8,12},{12,8},{16,20},{20,16},{24,28},{28,24},{1,5},{5... | collective-permute-start | bytes 12582920 | tf_op jit(solution)/shard_map/ppermute | solution.py:35
  229.5 28.6 %collective-permute-start.31 = (bf16[2,512,1024]{2,1,0:T(8,128)(2,1)S(1)}, bf16[2,512,1024]{2,1,0:T(8,128)(2,1)S(1)}, u32[]{:S(2)}, u32[]{:S(2)}) collective-permute-start(bf16[2,512,1024]{2,1,0:T(8,128)(2,1)S(1)} %copy-done.79), channel_id=1, source_target_pairs={{4,0},{8,4},{12,8},{16,12},{20,16},{24,20},{28,24},{5,1},{9,5},{13... | collective-permute-start | bytes 6291464 | tf_op jit(solution)/shard_map/ppermute | solution.py:41
  230.8 24.5 %collective-permute-start.29 = (bf16[512,1024]{1,0:T(8,128)(2,1)S(1)}, bf16[512,1024]{1,0:T(8,128)(2,1)S(1)}, u32[]{:S(2)}, u32[]{:S(2)}) collective-permute-start(bf16[512,1024]{1,0:T(8,128)(2,1)S(1)} %shard_map.296), channel_id=1, source_target_pairs={{0,1},{3,2},{4,5},{7,6},{8,9},{11,10},{12,13},{15,14},{16,17},{19,... | collective-permute-start | bytes 3145736 | tf_op jit(solution)/shard_map/ppermute | solution.py:1203
  232.1 24.5 %collective-permute-start.30 = (bf16[512,1024]{1,0:T(8,128)(2,1)S(1)}, bf16[512,1024]{1,0:T(8,128)(2,1)S(1)}, u32[]{:S(2)}, u32[]{:S(2)}) collective-permute-start(bf16[512,1024]{1,0:T(8,128)(2,1)S(1)} %add_convert_fusion.3), channel_id=1, source_target_pairs={{1,2},{2,1},{5,6},{6,5},{9,10},{10,9},{13,14},{14,13},{17,18},{18,... | collective-permute-start | bytes 3145736 | tf_op jit(solution)/shard_map/ppermute | solution.py:1203
  264.1 18.7 %collective-permute-start.33 = (bf16[512,1024]{1,0:T(8,128)(2,1)}, bf16[512,1024]{1,0:T(8,128)(2,1)}, u32[]{:S(2)}, u32[]{:S(2)}) collective-permute-start(bf16[512,1024]{1,0:T(8,128)(2,1)} %add_convert_fusion.2), channel_id=1, source_target_pairs={{1,2},{2,1},{5,6},{6,5},{9,10},{10,9},{13,14},{14,13},{17,18},{18,... | collective-permute-start | bytes 3145736 | tf_op jit(solution)/shard_map/ppermute | solution.py:1203
  265.8 32.3 %collective-permute-start.35 = (bf16[2,256,1024]{2,1,0:T(8,128)(2,1)}, bf16[2,256,1024]{2,1,0:T(8,128)(2,1)}, u32[]{:S(2)}, u32[]{:S(2)}) collective-permute-start(bf16[2,256,1024]{2,1,0:T(8,128)(2,1)} %get-tuple-element.334), channel_id=1, source_target_pairs={{0,16},{4,20},{8,24},{12,28},{16,0},{20,4},{24,8},{28,12},{1,17},{... | collective-permute-start | bytes 3145736 | tf_op jit(solution)/shard_map/ppermute | solution.py:35
  267.9 30.2 %collective-permute-start.34 = (bf16[2,256,1024]{2,1,0:T(8,128)(2,1)}, bf16[2,256,1024]{2,1,0:T(8,128)(2,1)}, u32[]{:S(2)}, u32[]{:S(2)}) collective-permute-start(bf16[2,256,1024]{2,1,0:T(8,128)(2,1)} %get-tuple-element.331), channel_id=1, source_target_pairs={{0,8},{4,12},{8,0},{12,4},{16,24},{20,28},{24,16},{28,20},{1,9},{5... | collective-permute-start | bytes 3145736 | tf_op jit(solution)/shard_map/ppermute | solution.py:35
  268.6 33.0 %collective-permute-start.36 = (bf16[512,1024]{1,0:T(8,128)(2,1)}, bf16[512,1024]{1,0:T(8,128)(2,1)}, u32[]{:S(2)}, u32[]{:S(2)}) collective-permute-start(bf16[512,1024]{1,0:T(8,128)(2,1)} %add_convert_fusion.1), channel_id=1, source_target_pairs={{1,0},{2,3},{5,4},{6,7},{9,8},{10,11},{13,12},{14,15},{17,16},{18,... | collective-permute-start | bytes 3145736 | tf_op jit(solution)/shard_map/ppermute | solution.py:1203
  286.4 22.6 %collective-permute-start.38 = (bf16[2,192,1024]{2,1,0:T(8,128)(2,1)S(1)}, bf16[2,192,1024]{2,1,0:T(8,128)(2,1)S(1)}, u32[]{:S(2)}, u32[]{:S(2)}) collective-permute-start(bf16[2,192,1024]{2,1,0:T(8,128)(2,1)S(1)} %get-tuple-element.344), channel_id=1, source_target_pairs={{0,16},{4,20},{8,24},{12,28},{16,0},{20,4},{24,8},{28,12},{1,17},{... | collective-permute-start | bytes 2359304 | tf_op jit(solution)/shard_map/ppermute | solution.py:35
  288.7 22.3 %collective-permute-start.37 = (bf16[2,192,1024]{2,1,0:T(8,128)(2,1)S(1)}, bf16[2,192,1024]{2,1,0:T(8,128)(2,1)S(1)}, u32[]{:S(2)}, u32[]{:S(2)}) collective-permute-start(bf16[2,192,1024]{2,1,0:T(8,128)(2,1)S(1)} %get-tuple-element.341), channel_id=1, source_target_pairs={{0,8},{4,12},{8,0},{12,4},{16,24},{20,28},{24,16},{28,20},{1,9},{5... | collective-permute-start | bytes 2359304 | tf_op jit(solution)/shard_map/ppermute | solution.py:35
  300.2 21.3 %collective-permute-start.40 = (bf16[256,1024]{1,0:T(8,128)(2,1)S(1)}, bf16[256,1024]{1,0:T(8,128)(2,1)S(1)}, u32[]{:S(2)}, u32[]{:S(2)}) collective-permute-start(bf16[256,1024]{1,0:T(8,128)(2,1)S(1)} %get-tuple-element.349), channel_id=1, source_target_pairs={{0,8},{4,12},{8,0},{12,4},{16,24},{20,28},{24,16},{28,20},{1,9},{5... | collective-permute-start | bytes 1572872 | tf_op jit(solution)/shard_map/ppermute | solution.py:35
  301.5 20.8 %collective-permute-start.39 = (bf16[256,1024]{1,0:T(8,128)(2,1)S(1)}, bf16[256,1024]{1,0:T(8,128)(2,1)}, u32[]{:S(2)}, u32[]{:S(2)}) collective-permute-start(bf16[256,1024]{1,0:T(8,128)(2,1)S(1)} %get-tuple-element.347), channel_id=1, source_target_pairs={{0,16},{4,20},{8,24},{12,28},{16,0},{20,4},{24,8},{28,12},{1,17},{... | collective-permute-start | bytes 1572872 | tf_op jit(solution)/shard_map/ppermute | solution.py:35
  326.0 37.7 %collective-permute-start.55 = (bf16[512,1024]{1,0:T(8,128)(2,1)S(1)}, bf16[512,1024]{1,0:T(8,128)(2,1)S(1)}, u32[]{:S(2)}, u32[]{:S(2)}) collective-permute-start(bf16[512,1024]{1,0:T(8,128)(2,1)S(1)} %copy-done.90), channel_id=1, source_target_pairs={{1,0},{2,3},{5,4},{6,7},{9,8},{10,11},{13,12},{14,15},{17,16},{18,... | collective-permute-start | bytes 3145736 | tf_op jit(solution)/shard_map/ppermute | solution.py:1203
  327.3 20.4 %collective-permute-start.42 = (bf16[192,1024]{1,0:T(8,128)(2,1)S(1)}, bf16[192,1024]{1,0:T(8,128)(2,1)S(1)}, u32[]{:S(2)}, u32[]{:S(2)}) collective-permute-start(bf16[192,1024]{1,0:T(8,128)(2,1)S(1)} %get-tuple-element.353), channel_id=1, source_target_pairs={{0,8},{4,12},{8,0},{12,4},{16,24},{20,28},{24,16},{28,20},{1,9},{5... | collective-permute-start | bytes 1179656 | tf_op jit(solution)/shard_map/ppermute | solution.py:35
  328.7 19.1 %collective-permute-start.41 = (bf16[192,1024]{1,0:T(8,128)(2,1)S(1)}, bf16[192,1024]{1,0:T(8,128)(2,1)S(1)}, u32[]{:S(2)}, u32[]{:S(2)}) collective-permute-start(bf16[192,1024]{1,0:T(8,128)(2,1)S(1)} %get-tuple-element.351), channel_id=1, source_target_pairs={{0,16},{4,20},{8,24},{12,28},{16,0},{20,4},{24,8},{28,12},{1,17},{... | collective-permute-start | bytes 1179656 | tf_op jit(solution)/shard_map/ppermute | solution.py:35
  328.9 24.1 %collective-permute-start.46 = (bf16[256,1024]{1,0:T(8,128)(2,1)S(1)}, bf16[256,1024]{1,0:T(8,128)(2,1)S(1)}, u32[]{:S(2)}, u32[]{:S(2)}) collective-permute-start(bf16[256,1024]{1,0:T(8,128)(2,1)S(1)} %get-tuple-element.359), channel_id=1, source_target_pairs={{0,1},{3,2},{4,5},{7,6},{8,9},{11,10},{12,13},{15,14},{16,17},{19,... | collective-permute-start | bytes 1572872 | tf_op jit(solution)/shard_map/ppermute | solution.py:1203
  342.4 19.7 %collective-permute-start.47 = (bf16[256,1024]{1,0:T(8,128)(2,1)S(1)}, bf16[256,1024]{1,0:T(8,128)(2,1)S(1)}, u32[]{:S(2)}, u32[]{:S(2)}) collective-permute-start(bf16[256,1024]{1,0:T(8,128)(2,1)S(1)} %get-tuple-element.362), channel_id=1, source_target_pairs={{0,1},{3,2},{4,5},{7,6},{8,9},{11,10},{12,13},{15,14},{16,17},{19,... | collective-permute-start | bytes 1572872 | tf_op jit(solution)/shard_map/ppermute | solution.py:1203
  351.7 24.7 %collective-permute-start.48 = (bf16[392,1024]{1,0:T(8,128)(2,1)S(1)}, bf16[392,1024]{1,0:T(8,128)(2,1)S(1)}, u32[]{:S(2)}, u32[]{:S(2)}) collective-permute-start(bf16[392,1024]{1,0:T(8,128)(2,1)S(1)} %pad_maximum_fusion.2), channel_id=1, source_target_pairs={{0,1},{3,2},{4,5},{7,6},{8,9},{11,10},{12,13},{15,14},{16,17},{19,... | collective-permute-start | bytes 2408456 | tf_op jit(solution)/shard_map/ppermute | solution.py:1203
  362.3 15.3 %collective-permute-start.49 = (bf16[256,1024]{1,0:T(8,128)(2,1)S(1)}, bf16[256,1024]{1,0:T(8,128)(2,1)S(1)}, u32[]{:S(2)}, u32[]{:S(2)}) collective-permute-start(bf16[256,1024]{1,0:T(8,128)(2,1)S(1)} %add_convert_fusion.9), channel_id=1, source_target_pairs={{1,2},{2,1},{5,6},{6,5},{9,10},{10,9},{13,14},{14,13},{17,18},{18,... | collective-permute-start | bytes 1572872 | tf_op jit(solution)/shard_map/ppermute | solution.py:1203
  363.0 14.8 %collective-permute-start.50 = (bf16[256,1024]{1,0:T(8,128)(2,1)S(1)}, bf16[256,1024]{1,0:T(8,128)(2,1)S(1)}, u32[]{:S(2)}, u32[]{:S(2)}) collective-permute-start(bf16[256,1024]{1,0:T(8,128)(2,1)S(1)} %add_convert_fusion.8), channel_id=1, source_target_pairs={{1,2},{2,1},{5,6},{6,5},{9,10},{10,9},{13,14},{14,13},{17,18},{18,... | collective-permute-start | bytes 1572872 | tf_op jit(solution)/shard_map/ppermute | solution.py:1203
  378.0 21.7 %collective-permute-start.53 = (bf16[256,1024]{1,0:T(8,128)(2,1)S(1)}, bf16[256,1024]{1,0:T(8,128)(2,1)S(1)}, u32[]{:S(2)}, u32[]{:S(2)}) collective-permute-start(bf16[256,1024]{1,0:T(8,128)(2,1)S(1)} %add_convert_fusion.6), channel_id=1, source_target_pairs={{1,0},{2,3},{5,4},{6,7},{9,8},{10,11},{13,12},{14,15},{17,16},{18,... | collective-permute-start | bytes 1572872 | tf_op jit(solution)/shard_map/ppermute | solution.py:1203
  379.4 30.4 %collective-permute-start.54 = (bf16[256,1024]{1,0:T(8,128)(2,1)S(1)}, bf16[256,1024]{1,0:T(8,128)(2,1)S(1)}, u32[]{:S(2)}, u32[]{:S(2)}) collective-permute-start(bf16[256,1024]{1,0:T(8,128)(2,1)S(1)} %add_convert_fusion.7), channel_id=1, source_target_pairs={{1,0},{2,3},{5,4},{6,7},{9,8},{10,11},{13,12},{14,15},{17,16},{18,... | collective-permute-start | bytes 1572872 | tf_op jit(solution)/shard_map/ppermute | solution.py:1203
  382.5 40.0 %collective-permute-start.52 = (bf16[392,1024]{1,0:T(8,128)(2,1)S(1)}, bf16[392,1024]{1,0:T(8,128)(2,1)S(1)}, u32[]{:S(2)}, u32[]{:S(2)}) collective-permute-start(bf16[392,1024]{1,0:T(8,128)(2,1)S(1)} %add_convert_fusion.4), channel_id=1, source_target_pairs={{1,0},{2,3},{5,4},{6,7},{9,8},{10,11},{13,12},{14,15},{17,16},{18,... | collective-permute-start | bytes 2408456 | tf_op jit(solution)/shard_map/ppermute | solution.py:1203
  (125 other events, 1549.1 us)

commit v2 on v1

--- a/solution.py
+++ b/solution.py
@@ -1029,6 +1029,8 @@
         plans.append(plan)
         sizes.append(total)
         start += total
+    if extras and recv is not None:
+        args = [pltpu.with_memory_space_constraint(arg, pltpu.HBM) for arg in args]
     args = lefts + args + list(extras)
     specs = [fixed(left.shape) for left in lefts] + specs + [fixed(e.shape) for e in extras]
     merge = recv is not None

time: 434 us -> 433 us (level)
  transfers between devices with their start and end apart: 56 -> 56, of which waited for: 26 -> 27; matrix products, arithmetic and copies ran while one was open for 4% -> 4% of each run, Pallas kernels for 33% -> 34%
where the time goes in v2:
time: 433 us; the launch traced here: 425 us
  Pallas kernels  195 us (45%)
  waiting for transfers between devices  110 us (25%)
  starting transfers between devices  73.9 us (17%)
  local copies, waits for them, and re-layouts  29 us (7%)
  other arithmetic  13.6 us (3%)
    pallas_call x35, Pallas kernels, run(): pl.pallas_call(kernel, out_shape=outs, grid_spec=pltpu.PrefetchScalarGrid...  195 us
    ppermute x15, waiting for transfers between devices, send(): self.recv = lax.ppermute(clock.at(self.value), 'dp', self.rounds[0][0])  56.3 us
    ppermute x39, waiting for transfers between devices, swapped(): lax.ppermute(value, axis, [(place, place ^ distance) for place in range(c...  54.2 us
    ppermute x39, starting transfers between devices, swapped(): lax.ppermute(value, axis, [(place, place ^ distance) for place in range(c...  38.2 us
    ppermute x15, starting transfers between devices, send(): self.recv = lax.ppermute(clock.at(self.value), 'dp', self.rounds[0][0])  32 us
    unnamed x215, local copies, waits for them, and re-layouts  24.6 us
  transfers between devices with their start and end apart: 56, of which 27 were waited for; matrix products, arithmetic and copies ran while one was open for 4% of the time, Pallas kernels for 34%

profile of v2, /device:TPU:0, one launch (start us, length us, event | category | flops | bytes accessed | tf_op | source)
XLA Modules:
  0.0 425.2 jit_solution(14494125088425884753)
XLA Ops:
  5.7 7.3 %shard_map.271 = (bf16[512,1024]{1,0:T(8,128)(2,1)S(1)}, bf16[512,1024]{1,0:T(8,128)(2,1)S(1)}, bf16[2,512,1024]{2,1,0:T(8,128)(2,1)S(1)}) custom-call(s32[3]{0:T(128)S(1)} %pad_add_fusion.flags, bf16[512,1024]{1,0:T(8,128)(2,1)S(1)} %bitcast.72, f32[1,1024]{1,0:T(1,128)S(1)} %bitcast.80, bf16[1024,1024]{1,0:T(8,128)(2,1)} %wq.3, bf16[1024,1024]{1,0:T(8,128)(2,1)} %wk.9, ...), custom_call_target="tpu_custom_call" | custom-call | flops 3221225472 | bytes 11538432 | tf_op jit(solution)/shard_map/pallas_call | solution.py:103
  14.1 10.9 %shard_map.272 = (bf16[512,1024]{1,0:T(8,128)(2,1)S(1)}, f32[512,1024]{1,0:T(8,128)S(1)}, f32[512,1024]{1,0:T(8,128)S(1)}, bf16[2,256,1024]{2,1,0:T(8,128)(2,1)S(1)}, bf16[2,256,1024]{2,1,0:T(8,128)(2,1)S(1)}) custom-call(s32[3]{0:T(128)S(1)} %pad_add_fusion.flags, bf16[512,1024]{1,0:T(8,128)(2,1)S(1)} %copy-done.65, ...), custom_call_target="tpu_custom_call" | custom-call | flops 3221225472 | bytes 20975616 | tf_op jit(solution)/shard_map/pallas_call | solution.py:103
  27.6 4.6 %shard_map.273.refs_1_.left = bf16[2,512,1024]{2,1,0:T(8,128)(2,1)S(1)} custom-call(s32[3]{0:T(128)S(1)} %pad_add_fusion.flags, bf16[512,1024]{1,0:T(8,128)(2,1)S(1)} %collective-permute-done.tokens, f32[1,1024]{1,0:T(1,128)S(1)} %bitcast.81, bf16[1024,1024]{1,0:T(8,128)(2,1)S(1)} %copy-done.8, bf16[1024,1024]{1,0:T(8,128)(2,1)S(1)} %copy-done.11), custom_call_target="tpu_custom_call" | custom-call | flops 99999997952 | bytes 7344128 | tf_op jit(solution)/shard_map/pallas_call | solution.py:103
  38.6 6.6 %shard_map.275 = (bf16[512,2048]{1,0:T(8,128)(2,1)S(1)}, bf16[512,2048]{1,0:T(8,128)(2,1)S(1)}) custom-call(s32[3]{0:T(128)S(1)} %pad_add_fusion.flags, bf16[512,1024]{1,0:T(8,128)(2,1)S(1)} %bitcast.61, bf16[8,512,1024]{2,1,0:T(8,128)(2,1)S(1)} %bitcast.59, bf16[8,512,1024]{2,1,0:T(8,128)(2,1)S(1)} %bitcast.60), custom_call_target="tpu_custom_call" | custom-call | flops 4294967296 | bytes 22020096 | tf_op jit(solution)/shard_map/pallas_call | solution.py:103
  45.2 5.0 %collective-permute-done.3.from2.kept2 = bf16[2,64,1024]{2,1,0:T(8,128)(2,1)S(1)} collective-permute-done((bf16[2,64,1024]{2,1,0:T(8,128)(2,1)S(1)}, bf16[2,64,1024]{2,1,0:T(8,128)(2,1)S(1)}, u32[]{:S(2)}, u32[]{:S(2)}) %collective-permute-start.3) | collective-permute-done | bytes 262176 | tf_op jit(solution)/shard_map/ppermute | solution.py:35
  62.7 5.5 %shard_map.278 = (f32[512,1024]{1,0:T(8,128)S(1)}, bf16[512,1024]{1,0:T(8,128)(2,1)S(1)}, f32[512,1024]{1,0:T(8,128)}, bf16[2,512,1024]{2,1,0:T(8,128)(2,1)S(1)}) custom-call(s32[3]{0:T(128)S(1)} %pad_add_fusion.flags, bf16[256,1024]{1,0:T(8,128)(2,1)S(1)} %get-tuple-element.219.mine, bf16[256,1024]{1,0:T(8,128)(2,1)S(1)} %collective-permute-done.8.other, ...), custom_call_target="tpu_custom_call" | custom-call | flops 2147483648 | bytes 18874368 | tf_op jit(solution)/shard_map/pallas_call | solution.py:103
  69.5 14.3 %shard_map.279 = (bf16[512,1024]{1,0:T(8,128)(2,1)S(1)}, f32[8,1,512]{2,1,0:T(1,128)S(1)}) custom-call(s32[3]{0:T(128)S(1)} %pad_add_fusion.flags, bf16[512,1024]{1,0:T(8,128)(2,1)} %copy-done.85, bf16[2,512,1024]{2,1,0:T(8,128)(2,1)} %copy-done.84, bf16[2,512,1024]{2,1,0:T(8,128)(2,1)} %copy-done.53, bf16[2,512,1024]{2,1,0:T(8,128)(2,1)} %copy-done.80), custom_call_target="tpu_custom_call" | custom-call | flops 3221225472 | bytes 8404992 | tf_op jit(solution)/shard_map/pallas_call | solution.py:103
  83.8 13.4 %shard_map.280 = (bf16[512,2048]{1,0:T(8,128)(2,1)S(1)}, bf16[512,2048]{1,0:T(8,128)(2,1)S(1)}, bf16[512,1024]{1,0:T(8,128)(2,1)S(1)}, f32[512,1024]{1,0:T(8,128...) custom-call(s32[3]{0:T(128)S(1)} %pad_add_fusion.flags, ...), custom_call_target="tpu_custom_call" | custom-call | flops 7516192768 | bytes 42995712 | tf_op jit(solution)/shard_map/pallas_call | solution.py:103
  100.0 3.6 shard_map.281
  103.7 7.0 %collective-permute-done.9.refs_4_ = bf16[4,512,1024]{2,1,0:T(8,128)(2,1)S(1)} collective-permute-done((bf16[4,512,1024]{2,1,0:T(8,128)(2,1)S(1)}, bf16[4,512,1024]{2,1,0:T(8,128)(2,1)S(1)}, u32[]{:S(2)}, u32[]{:S(2)}) %collective-permute-start.9) | collective-permute-done | bytes 4194336 | tf_op jit(solution)/shard_map/ppermute | solution.py:35
  110.8 4.5 %shard_map.282 = (bf16[2,256,1024]{2,1,0:T(8,128)(2,1)S(1)}, bf16[2,256,1024]{2,1,0:T(8,128)(2,1)S(1)}, bf16[2,256,1024]{2,1,0:T(8,128)(2,1)}, bf16[2,256,1024]{2,1,0:T(8,128)(2,1)S(1)}) custom-call(s32[3]{0:T(128)S(1)} %pad_add_fusion.flags, bf16[512,2048]{1,0:T(8,128)(2,1)S(1)} %get-tuple-element.230.refs_0_, ...), custom_call_target="tpu_custom_call" | custom-call | flops 2147483648 | bytes 14680064 | tf_op jit(solution)/shard_map/pallas_call | solution.py:103
  120.5 15.9 %shard_map.283 = (bf16[512,2048]{1,0:T(8,128)(2,1)S(1)}, bf16[512,2048]{1,0:T(8,128)(2,1)S(1)}, bf16[512,1024]{1,0:T(8,128)(2,1)}, f32[512,1024]{1,0:T(8,128)S(1...) custom-call(s32[3]{0:T(128)S(1)} %pad_add_fusion.flags, ...), custom_call_target="tpu_custom_call" | custom-call | flops 7516192768 | bytes 47194112 | tf_op jit(solution)/shard_map/pallas_call | solution.py:103
  136.4 3.6 shard_map.284
  147.2 4.6 %shard_map.286 = (bf16[2,256,1024]{2,1,0:T(8,128)(2,1)S(1)}, bf16[2,256,1024]{2,1,0:T(8,128)(2,1)S(1)}, bf16[2,256,1024]{2,1,0:T(8,128)(2,1)}, bf16[2,256,1024]{2,1,0:T(8,128)(2,1)S(1)}) custom-call(s32[3]{0:T(128)S(1)} %pad_add_fusion.flags, bf16[512,2048]{1,0:T(8,128)(2,1)S(1)} %get-tuple-element.244.refs_0_, ...), custom_call_target="tpu_custom_call" | custom-call | flops 2147483648 | bytes 14680064 | tf_op jit(solution)/shard_map/pallas_call | solution.py:103
  153.8 23.0 %shard_map.287 = (bf16[512,1024]{1,0:T(8,128)(2,1)S(1)}, bf16[2,512,1024]{2,1,0:T(8,128)(2,1)S(1)}, f32[2,512,1024]{2,1,0:T(8,128)S(1)}, bf16[2,512,1024]{2,1,0:T(8,128)(2,1)S(1)}) custom-call(s32[3]{0:T(128)S(1)} %pad_add_fusion.flags, bf16[512,1024]{1,0:T(8,128)(2,1)} %copy-done.85, bf16[2,512,1024]{2,1,0:T(8,128)(2,1)} %copy-done.84, ...), custom_call_target="tpu_custom_call" | custom-call | flops 8053063680 | bytes 17842176 | tf_op jit(solution)/shard_map/pallas_call | solution.py:103
  176.9 4.3 %shard_map.288 = (f32[512,1024]{1,0:T(8,128)S(1)}, bf16[256,1024]{1,0:T(8,128)(2,1)S(1)}, bf16[256,1024]{1,0:T(8,128)(2,1)S(1)}) custom-call(s32[3]{0:T(128)S(1)} %pad_add_fusion.flags, bf16[2,512,1024]{2,1,0:T(8,128)(2,1)S(1)} %get-tuple-element.262.state_grad.refs_4_.refs_7_, bf16[1024,1024]{1,0:T(8,128)(2,1)S(1)} %copy-done.9, ...), custom_call_target="tpu_custom_call" | custom-call | flops 2147483648 | bytes 13631488 | tf_op jit(solution)/shard_map/pallas_call | solution.py:103
  213.4 6.9 %shard_map.294 = (bf16[512,1024]{1,0:T(8,128)(2,1)S(1)}, bf16[2,512,1024]{2,1,0:T(8,128)(2,1)S(1)}, f32[1,1024]{1,0:T(1,128)S(1)}, bf16[512,1024]{1,0:T(8,128)(2,1)S(1)}) custom-call(s32[3]{0:T(128)S(1)} %pad_add_fusion.flags, bf16[256,1024]{1,0:T(8,128)(2,1)S(1)} %get-tuple-element.288.mine, bf16[256,1024]{1,0:T(8,128)(2,1)S(1)} %collective-permute-done.25.other, ...), custom_call_target="tpu_custom_call" | custom-call | flops 2147483648 | bytes 24121344 | tf_op jit(solution)/shard_map/pallas_call | solution.py:103
  220.3 3.7 shard_map.295
  232.9 12.3 %shard_map.297 = (bf16[512,1024]{1,0:T(8,128)(2,1)S(1)}, bf16[2,512,1024]{2,1,0:T(8,128)(2,1)S(1)}) custom-call(s32[3]{0:T(128)S(1)} %pad_add_fusion.flags, bf16[512,1024]{1,0:T(8,128)(2,1)} %refs_0_.1, bf16[2,512,1024]{2,1,0:T(8,128)(2,1)} %copy-done.53, bf16[512,1024]{1,0:T(8,128)(2,1)} %copy-done.82, f32[2,512,1024]{2,1,0:T(8,128)} %copy-done.83), custom_call_target="tpu_custom_call" | custom-call | flops 2684354560 | bytes 11534336 | tf_op jit(solution)/shard_map/pallas_call | solution.py:103
  249.8 5.0 %shard_map.298 = (bf16[2,256,1024]{2,1,0:T(8,128)(2,1)}, bf16[2,256,1024]{2,1,0:T(8,128)(2,1)S(1)}, bf16[2,256,1024]{2,1,0:T(8,128)(2,1)}, bf16[2,256,1024]{2,1,0:T(8,128)(2,1)S(1)}) custom-call(s32[3]{0:T(128)S(1)} %pad_add_fusion.flags, bf16[512,1024]{1,0:T(8,128)(2,1)S(1)} %get-tuple-element.228.attended.refs_0_, bf16[512,1024]{1,0:T(8,128)(2,1)S(1)} %copy-done.47, ...), custom_call_target="tpu_custom_call" | custom-call | flops 2147483648 | bytes 17825792 | tf_op jit(solution)/shard_map/pallas_call | solution.py:103
  258.1 5.0 %shard_map.299 = bf16[4,384,1024]{2,1,0:T(8,128)(2,1)} custom-call(s32[3]{0:T(128)S(1)} %pad_add_fusion.flags, bf16[512,1024]{1,0:T(8,128)(2,1)S(1)} %get-tuple-element.199.refs_2_.refs_0_, bf16[512,1024]{1,0:T(8,128)(2,1)S(1)} %get-tuple-element.316.refs_1_, bf16[2,512,1024]{2,1,0:T(8,128)(2,1)S(1)} %get-tuple-element.317.refs_2_.refs_5_.pair_total, ...), custom_call_target="tpu_custom_call" | custom-call | flops 3221225472 | bytes 19922944 | tf_op jit(solution)/shard_map/pallas_call | solution.py:103
  273.4 7.8 %shard_map.300 = (bf16[2,192,1024]{2,1,0:T(8,128)(2,1)S(1)}, bf16[2,192,1024]{2,1,0:T(8,128)(2,1)S(1)}, bf16[2,192,1024]{2,1,0:T(8,128)(2,1)S(1)}, bf16[2,192,1024]{2,1,0:T(8,128)(2,1)S(1)}) custom-call(s32[3]{0:T(128)S(1)} %pad_add_fusion.flags, bf16[512,1024]{1,0:T(8,128)(2,1)S(1)} %get-tuple-element.199.refs_2_.refs_0_, bf16[512,1024]{1,0:T(8,128)(2,1)S(1)} %copy-done.31, ...), custom_call_target="tpu_custom_call" | custom-call | flops 3221225472 | bytes 23068672 | tf_op jit(solution)/shard_map/pallas_call | solution.py:103
  287.8 8.7 %shard_map.301 = (f32[512,1024]{1,0:T(8,128)}, f32[1,1024]{1,0:T(1,128)S(1)}) custom-call(s32[3]{0:T(128)S(1)} %pad_add_fusion.flags, bf16[512,1024]{1,0:T(8,128)(2,1)S(1)} %copy-done.21, bf16[2,512,1024]{2,1,0:T(8,128)(2,1)S(1)} %copy-done.5, bf16[2,512,1024]{2,1,0:T(8,128)(2,1)S(1)} %copy-done.3, bf16[1024,1024]{1,0:T(8,128)(2,1)S(1)} %copy-done.52, ...), custom_call_target="tpu_custom_call" | custom-call | flops 3221225472 | bytes 16785408 | tf_op jit(solution)/shard_map/pallas_call | solution.py:103
  303.5 4.5 %collective-permute-done.38.recv2.refs_4_ = bf16[2,192,1024]{2,1,0:T(8,128)(2,1)S(1)} collective-permute-done((bf16[2,192,1024]{2,1,0:T(8,128)(2,1)S(1)}, bf16[2,192,1024]{2,1,0:T(8,128)(2,1)S(1)}, u32[]{:S(2)}, u32[]{:S(2)}) %collective-permute-start.38) | collective-permute-done | bytes 786464 | tf_op jit(solution)/shard_map/ppermute | solution.py:35
  311.1 9.5 %collective-permute-done.40.refs_5_ = bf16[256,1024]{1,0:T(8,128)(2,1)S(1)} collective-permute-done((bf16[256,1024]{1,0:T(8,128)(2,1)}, bf16[256,1024]{1,0:T(8,128)(2,1)S(1)}, u32[]{:S(2)}, u32[]{:S(2)}) %collective-permute-start.40) | collective-permute-done | bytes 524320 | tf_op jit(solution)/shard_map/ppermute | solution.py:35
  328.1 10.1 %collective-permute-start.46 = (bf16[256,1024]{1,0:T(8,128)(2,1)S(1)}, bf16[256,1024]{1,0:T(8,128)(2,1)S(1)}, u32[]{:S(2)}, u32[]{:S(2)}) collective-permute-start(bf16[256,1024]{1,0:T(8,128)(2,1)S(1)} %get-tuple-element.359), channel_id=1, source_target_pairs={{0,1},{3,2},{4,5},{7,6},{8,9},{11,10},{12,13},{15,14},{16,17},{19,... | collective-permute-start | bytes 1572872 | tf_op jit(solution)/shard_map/ppermute | solution.py:1205
  342.1 5.4 %collective-permute-start.47 = (bf16[256,1024]{1,0:T(8,128)(2,1)S(1)}, bf16[256,1024]{1,0:T(8,128)(2,1)S(1)}, u32[]{:S(2)}, u32[]{:S(2)}) collective-permute-start(bf16[256,1024]{1,0:T(8,128)(2,1)S(1)} %get-tuple-element.362), channel_id=1, source_target_pairs={{0,1},{3,2},{4,5},{7,6},{8,9},{11,10},{12,13},{15,14},{16,17},{19,... | collective-permute-start | bytes 1572872 | tf_op jit(solution)/shard_map/ppermute | solution.py:1205
  353.0 8.7 %collective-permute-done.47 = bf16[256,1024]{1,0:T(8,128)(2,1)S(1)} collective-permute-done((bf16[256,1024]{1,0:T(8,128)(2,1)S(1)}, bf16[256,1024]{1,0:T(8,128)(2,1)S(1)}, u32[]{:S(2)}, u32[]{:S(2)}) %collective-permute-start.47) | collective-permute-done | bytes 524320 | tf_op jit(solution)/shard_map/ppermute | solution.py:1205
  364.9 11.3 %collective-permute-done.48 = bf16[392,1024]{1,0:T(8,128)(2,1)S(1)} collective-permute-done((bf16[392,1024]{1,0:T(8,128)(2,1)S(1)}, bf16[392,1024]{1,0:T(8,128)(2,1)S(1)}, u32[]{:S(2)}, u32[]{:S(2)}) %collective-permute-start.48) | collective-permute-done | bytes 802848 | tf_op jit(solution)/shard_map/ppermute | solution.py:1205
  383.6 16.0 %collective-permute-done.53 = bf16[256,1024]{1,0:T(8,128)(2,1)S(1)} collective-permute-done((bf16[256,1024]{1,0:T(8,128)(2,1)S(1)}, bf16[256,1024]{1,0:T(8,128)(2,1)S(1)}, u32[]{:S(2)}, u32[]{:S(2)}) %collective-permute-start.53) | collective-permute-done | bytes 524320 | tf_op jit(solution)/shard_map/ppermute | solution.py:1205
  399.6 10.1 %collective-permute-done.54 = bf16[256,1024]{1,0:T(8,128)(2,1)S(1)} collective-permute-done((bf16[256,1024]{1,0:T(8,128)(2,1)S(1)}, bf16[256,1024]{1,0:T(8,128)(2,1)S(1)}, u32[]{:S(2)}, u32[]{:S(2)}) %collective-permute-start.54) | collective-permute-done | bytes 524320 | tf_op jit(solution)/shard_map/ppermute | solution.py:1205
  412.6 9.8 %collective-permute-done.52 = bf16[392,1024]{1,0:T(8,128)(2,1)S(1)} collective-permute-done((bf16[392,1024]{1,0:T(8,128)(2,1)S(1)}, bf16[392,1024]{1,0:T(8,128)(2,1)S(1)}, u32[]{:S(2)}, u32[]{:S(2)}) %collective-permute-start.52) | collective-permute-done | bytes 802848 | tf_op jit(solution)/shard_map/ppermute | solution.py:1205
  (372 shorter events, 153.4 us)
Async XLA Ops:
  0.6 27.0 %collective-permute-start = (bf16[512,1024]{1,0:T(8,128)(2,1)}, bf16[512,1024]{1,0:T(8,128)(2,1)S(1)}, u32[]{:S(2)}, u32[]{:S(2)}) collective-permute-start(bf16[512,1024]{1,0:T(8,128)(2,1)} %bitcast.71), channel_id=1, source_target_pairs={{0,4},{4,8},{8,12},{12,16},{16,20},{20,24},{24,28},{1,5},{5,9},{9,... | collective-permute-start | bytes 3145736 | tf_op jit(solution)/shard_map/ppermute | solution.py:41
  115.3 25.4 %collective-permute-start.11 = (bf16[2,256,1024]{2,1,0:T(8,128)(2,1)}, bf16[2,256,1024]{2,1,0:T(8,128)(2,1)S(1)}, u32[]{:S(2)}, u32[]{:S(2)}) collective-permute-start(bf16[2,256,1024]{2,1,0:T(8,128)(2,1)} %get-tuple-element.252), channel_id=1, source_target_pairs={{0,16},{4,20},{8,24},{12,28},{16,0},{20,4},{24,8},{28,12},{1,17},{... | collective-permute-start | bytes 3145736 | tf_op jit(solution)/shard_map/ppermute | solution.py:35
  116.3 24.9 %collective-permute-start.10 = (bf16[2,256,1024]{2,1,0:T(8,128)(2,1)S(1)}, bf16[2,256,1024]{2,1,0:T(8,128)(2,1)S(1)}, u32[]{:S(2)}, u32[]{:S(2)}) collective-permute-start(bf16[2,256,1024]{2,1,0:T(8,128)(2,1)S(1)} %get-tuple-element.249), channel_id=1, source_target_pairs={{0,8},{4,12},{8,0},{12,4},{16,24},{20,28},{24,16},{28,20},{1,9},{5... | collective-permute-start | bytes 3145736 | tf_op jit(solution)/shard_map/ppermute | solution.py:35
  143.0 38.3 %collective-permute-start.14 = (bf16[256,1024]{1,0:T(8,128)(2,1)}, bf16[256,1024]{1,0:T(8,128)(2,1)}, u32[]{:S(2)}, u32[]{:S(2)}) collective-permute-start(bf16[256,1024]{1,0:T(8,128)(2,1)} %get-tuple-element.267), channel_id=1, source_target_pairs={{0,8},{4,12},{8,0},{12,4},{16,24},{20,28},{24,16},{28,20},{1,9},{5... | collective-permute-start | bytes 1572872 | tf_op jit(solution)/shard_map/ppermute | solution.py:35
  143.9 37.3 %collective-permute-start.13 = (bf16[256,1024]{1,0:T(8,128)(2,1)}, bf16[256,1024]{1,0:T(8,128)(2,1)}, u32[]{:S(2)}, u32[]{:S(2)}) collective-permute-start(bf16[256,1024]{1,0:T(8,128)(2,1)} %get-tuple-element.265), channel_id=1, source_target_pairs={{0,16},{4,20},{8,24},{12,28},{16,0},{20,4},{24,8},{28,12},{1,17},{... | collective-permute-start | bytes 1572872 | tf_op jit(solution)/shard_map/ppermute | solution.py:35
  151.7 41.2 %collective-permute-start.17 = (bf16[2,256,1024]{2,1,0:T(8,128)(2,1)}, bf16[2,256,1024]{2,1,0:T(8,128)(2,1)S(1)}, u32[]{:S(2)}, u32[]{:S(2)}) collective-permute-start(bf16[2,256,1024]{2,1,0:T(8,128)(2,1)} %get-tuple-element.277), channel_id=1, source_target_pairs={{0,16},{4,20},{8,24},{12,28},{16,0},{20,4},{24,8},{28,12},{1,17},{... | collective-permute-start | bytes 3145736 | tf_op jit(solution)/shard_map/ppermute | solution.py:35
  152.5 41.8 %collective-permute-start.16 = (bf16[2,256,1024]{2,1,0:T(8,128)(2,1)S(1)}, bf16[2,256,1024]{2,1,0:T(8,128)(2,1)S(1)}, u32[]{:S(2)}, u32[]{:S(2)}) collective-permute-start(bf16[2,256,1024]{2,1,0:T(8,128)(2,1)S(1)} %get-tuple-element.274), channel_id=1, source_target_pairs={{0,8},{4,12},{8,0},{12,4},{16,24},{20,28},{24,16},{28,20},{1,9},{5... | collective-permute-start | bytes 3145736 | tf_op jit(solution)/shard_map/ppermute | solution.py:35
  184.1 28.8 %collective-permute-start.24 = (bf16[512,1024]{1,0:T(8,128)(2,1)S(1)}, bf16[512,1024]{1,0:T(8,128)(2,1)S(1)}, u32[]{:S(2)}, u32[]{:S(2)}) collective-permute-start(bf16[512,1024]{1,0:T(8,128)(2,1)S(1)} %shard_map.289), channel_id=1, source_target_pairs={{0,1},{3,2},{4,5},{7,6},{8,9},{11,10},{12,13},{15,14},{16,17},{19,... | collective-permute-start | bytes 3145736 | tf_op jit(solution)/shard_map/ppermute | solution.py:1205
  210.7 14.3 %collective-permute-start.27 = (bf16[256,1024]{1,0:T(8,128)(2,1)S(1)}, bf16[256,1024]{1,0:T(8,128)(2,1)S(1)}, u32[]{:S(2)}, u32[]{:S(2)}) collective-permute-start(bf16[256,1024]{1,0:T(8,128)(2,1)S(1)} %get-tuple-element.301), channel_id=1, source_target_pairs={{0,8},{4,12},{8,0},{12,4},{16,24},{20,28},{24,16},{28,20},{1,9},{5... | collective-permute-start | bytes 1572872 | tf_op jit(solution)/shard_map/ppermute | solution.py:35
  229.4 15.8 %collective-permute-start.28 = (bf16[4,512,1024]{2,1,0:T(8,128)(2,1)S(1)}, bf16[4,512,1024]{2,1,0:T(8,128)(2,1)S(1)}, u32[]{:S(2)}, u32[]{:S(2)}) collective-permute-start(bf16[4,512,1024]{2,1,0:T(8,128)(2,1)S(1)} %shard_map.295), channel_id=1, source_target_pairs={{0,4},{4,0},{8,12},{12,8},{16,20},{20,16},{24,28},{28,24},{1,5},{5... | collective-permute-start | bytes 12582920 | tf_op jit(solution)/shard_map/ppermute | solution.py:35
  229.5 28.6 %collective-permute-start.31 = (bf16[2,512,1024]{2,1,0:T(8,128)(2,1)S(1)}, bf16[2,512,1024]{2,1,0:T(8,128)(2,1)S(1)}, u32[]{:S(2)}, u32[]{:S(2)}) collective-permute-start(bf16[2,512,1024]{2,1,0:T(8,128)(2,1)S(1)} %copy-done.79), channel_id=1, source_target_pairs={{4,0},{8,4},{12,8},{16,12},{20,16},{24,20},{28,24},{5,1},{9,5},{13... | collective-permute-start | bytes 6291464 | tf_op jit(solution)/shard_map/ppermute | solution.py:41
  230.8 24.5 %collective-permute-start.29 = (bf16[512,1024]{1,0:T(8,128)(2,1)S(1)}, bf16[512,1024]{1,0:T(8,128)(2,1)S(1)}, u32[]{:S(2)}, u32[]{:S(2)}) collective-permute-start(bf16[512,1024]{1,0:T(8,128)(2,1)S(1)} %shard_map.296), channel_id=1, source_target_pairs={{0,1},{3,2},{4,5},{7,6},{8,9},{11,10},{12,13},{15,14},{16,17},{19,... | collective-permute-start | bytes 3145736 | tf_op jit(solution)/shard_map/ppermute | solution.py:1205
  232.1 24.5 %collective-permute-start.30 = (bf16[512,1024]{1,0:T(8,128)(2,1)S(1)}, bf16[512,1024]{1,0:T(8,128)(2,1)S(1)}, u32[]{:S(2)}, u32[]{:S(2)}) collective-permute-start(bf16[512,1024]{1,0:T(8,128)(2,1)S(1)} %add_convert_fusion.3), channel_id=1, source_target_pairs={{1,2},{2,1},{5,6},{6,5},{9,10},{10,9},{13,14},{14,13},{17,18},{18,... | collective-permute-start | bytes 3145736 | tf_op jit(solution)/shard_map/ppermute | solution.py:1205
  264.1 17.3 %collective-permute-start.33 = (bf16[512,1024]{1,0:T(8,128)(2,1)}, bf16[512,1024]{1,0:T(8,128)(2,1)S(1)}, u32[]{:S(2)}, u32[]{:S(2)}) collective-permute-start(bf16[512,1024]{1,0:T(8,128)(2,1)} %add_convert_fusion.2), channel_id=1, source_target_pairs={{1,2},{2,1},{5,6},{6,5},{9,10},{10,9},{13,14},{14,13},{17,18},{18,... | collective-permute-start | bytes 3145736 | tf_op jit(solution)/shard_map/ppermute | solution.py:1205
  264.8 31.7 %collective-permute-start.35 = (bf16[2,256,1024]{2,1,0:T(8,128)(2,1)}, bf16[2,256,1024]{2,1,0:T(8,128)(2,1)}, u32[]{:S(2)}, u32[]{:S(2)}) collective-permute-start(bf16[2,256,1024]{2,1,0:T(8,128)(2,1)} %get-tuple-element.334), channel_id=1, source_target_pairs={{0,16},{4,20},{8,24},{12,28},{16,0},{20,4},{24,8},{28,12},{1,17},{... | collective-permute-start | bytes 3145736 | tf_op jit(solution)/shard_map/ppermute | solution.py:35
  267.0 29.6 %collective-permute-start.34 = (bf16[2,256,1024]{2,1,0:T(8,128)(2,1)}, bf16[2,256,1024]{2,1,0:T(8,128)(2,1)}, u32[]{:S(2)}, u32[]{:S(2)}) collective-permute-start(bf16[2,256,1024]{2,1,0:T(8,128)(2,1)} %get-tuple-element.331), channel_id=1, source_target_pairs={{0,8},{4,12},{8,0},{12,4},{16,24},{20,28},{24,16},{28,20},{1,9},{5... | collective-permute-start | bytes 3145736 | tf_op jit(solution)/shard_map/ppermute | solution.py:35
  267.7 33.1 %collective-permute-start.36 = (bf16[512,1024]{1,0:T(8,128)(2,1)}, bf16[512,1024]{1,0:T(8,128)(2,1)}, u32[]{:S(2)}, u32[]{:S(2)}) collective-permute-start(bf16[512,1024]{1,0:T(8,128)(2,1)} %add_convert_fusion.1), channel_id=1, source_target_pairs={{1,0},{2,3},{5,4},{6,7},{9,8},{10,11},{13,12},{14,15},{17,16},{18,... | collective-permute-start | bytes 3145736 | tf_op jit(solution)/shard_map/ppermute | solution.py:1205
  284.6 23.5 %collective-permute-start.38 = (bf16[2,192,1024]{2,1,0:T(8,128)(2,1)S(1)}, bf16[2,192,1024]{2,1,0:T(8,128)(2,1)S(1)}, u32[]{:S(2)}, u32[]{:S(2)}) collective-permute-start(bf16[2,192,1024]{2,1,0:T(8,128)(2,1)S(1)} %get-tuple-element.344), channel_id=1, source_target_pairs={{0,16},{4,20},{8,24},{12,28},{16,0},{20,4},{24,8},{28,12},{1,17},{... | collective-permute-start | bytes 2359304 | tf_op jit(solution)/shard_map/ppermute | solution.py:35
  287.1 23.0 %collective-permute-start.37 = (bf16[2,192,1024]{2,1,0:T(8,128)(2,1)S(1)}, bf16[2,192,1024]{2,1,0:T(8,128)(2,1)S(1)}, u32[]{:S(2)}, u32[]{:S(2)}) collective-permute-start(bf16[2,192,1024]{2,1,0:T(8,128)(2,1)S(1)} %get-tuple-element.341), channel_id=1, source_target_pairs={{0,8},{4,12},{8,0},{12,4},{16,24},{20,28},{24,16},{28,20},{1,9},{5... | collective-permute-start | bytes 2359304 | tf_op jit(solution)/shard_map/ppermute | solution.py:35
  299.4 21.2 %collective-permute-start.40 = (bf16[256,1024]{1,0:T(8,128)(2,1)}, bf16[256,1024]{1,0:T(8,128)(2,1)S(1)}, u32[]{:S(2)}, u32[]{:S(2)}) collective-permute-start(bf16[256,1024]{1,0:T(8,128)(2,1)} %get-tuple-element.349), channel_id=1, source_target_pairs={{0,8},{4,12},{8,0},{12,4},{16,24},{20,28},{24,16},{28,20},{1,9},{5... | collective-permute-start | bytes 1572872 | tf_op jit(solution)/shard_map/ppermute | solution.py:35
  300.8 20.6 %collective-permute-start.39 = (bf16[256,1024]{1,0:T(8,128)(2,1)}, bf16[256,1024]{1,0:T(8,128)(2,1)}, u32[]{:S(2)}, u32[]{:S(2)}) collective-permute-start(bf16[256,1024]{1,0:T(8,128)(2,1)} %get-tuple-element.347), channel_id=1, source_target_pairs={{0,16},{4,20},{8,24},{12,28},{16,0},{20,4},{24,8},{28,12},{1,17},{... | collective-permute-start | bytes 1572872 | tf_op jit(solution)/shard_map/ppermute | solution.py:35
  325.1 38.3 %collective-permute-start.55 = (bf16[512,1024]{1,0:T(8,128)(2,1)S(1)}, bf16[512,1024]{1,0:T(8,128)(2,1)S(1)}, u32[]{:S(2)}, u32[]{:S(2)}) collective-permute-start(bf16[512,1024]{1,0:T(8,128)(2,1)S(1)} %copy-done.90), channel_id=1, source_target_pairs={{1,0},{2,3},{5,4},{6,7},{9,8},{10,11},{13,12},{14,15},{17,16},{18,... | collective-permute-start | bytes 3145736 | tf_op jit(solution)/shard_map/ppermute | solution.py:1205
  326.4 21.1 %collective-permute-start.42 = (bf16[192,1024]{1,0:T(8,128)(2,1)S(1)}, bf16[192,1024]{1,0:T(8,128)(2,1)S(1)}, u32[]{:S(2)}, u32[]{:S(2)}) collective-permute-start(bf16[192,1024]{1,0:T(8,128)(2,1)S(1)} %get-tuple-element.353), channel_id=1, source_target_pairs={{0,8},{4,12},{8,0},{12,4},{16,24},{20,28},{24,16},{28,20},{1,9},{5... | collective-permute-start | bytes 1179656 | tf_op jit(solution)/shard_map/ppermute | solution.py:35
  327.8 19.7 %collective-permute-start.41 = (bf16[192,1024]{1,0:T(8,128)(2,1)S(1)}, bf16[192,1024]{1,0:T(8,128)(2,1)S(1)}, u32[]{:S(2)}, u32[]{:S(2)}) collective-permute-start(bf16[192,1024]{1,0:T(8,128)(2,1)S(1)} %get-tuple-element.351), channel_id=1, source_target_pairs={{0,16},{4,20},{8,24},{12,28},{16,0},{20,4},{24,8},{28,12},{1,17},{... | collective-permute-start | bytes 1179656 | tf_op jit(solution)/shard_map/ppermute | solution.py:35
  328.1 24.7 %collective-permute-start.46 = (bf16[256,1024]{1,0:T(8,128)(2,1)S(1)}, bf16[256,1024]{1,0:T(8,128)(2,1)S(1)}, u32[]{:S(2)}, u32[]{:S(2)}) collective-permute-start(bf16[256,1024]{1,0:T(8,128)(2,1)S(1)} %get-tuple-element.359), channel_id=1, source_target_pairs={{0,1},{3,2},{4,5},{7,6},{8,9},{11,10},{12,13},{15,14},{16,17},{19,... | collective-permute-start | bytes 1572872 | tf_op jit(solution)/shard_map/ppermute | solution.py:1205
  342.1 19.7 %collective-permute-start.47 = (bf16[256,1024]{1,0:T(8,128)(2,1)S(1)}, bf16[256,1024]{1,0:T(8,128)(2,1)S(1)}, u32[]{:S(2)}, u32[]{:S(2)}) collective-permute-start(bf16[256,1024]{1,0:T(8,128)(2,1)S(1)} %get-tuple-element.362), channel_id=1, source_target_pairs={{0,1},{3,2},{4,5},{7,6},{8,9},{11,10},{12,13},{15,14},{16,17},{19,... | collective-permute-start | bytes 1572872 | tf_op jit(solution)/shard_map/ppermute | solution.py:1205
  351.5 24.7 %collective-permute-start.48 = (bf16[392,1024]{1,0:T(8,128)(2,1)S(1)}, bf16[392,1024]{1,0:T(8,128)(2,1)S(1)}, u32[]{:S(2)}, u32[]{:S(2)}) collective-permute-start(bf16[392,1024]{1,0:T(8,128)(2,1)S(1)} %pad_maximum_fusion.2), channel_id=1, source_target_pairs={{0,1},{3,2},{4,5},{7,6},{8,9},{11,10},{12,13},{15,14},{16,17},{19,... | collective-permute-start | bytes 2408456 | tf_op jit(solution)/shard_map/ppermute | solution.py:1205
  362.0 15.4 %collective-permute-start.49 = (bf16[256,1024]{1,0:T(8,128)(2,1)S(1)}, bf16[256,1024]{1,0:T(8,128)(2,1)S(1)}, u32[]{:S(2)}, u32[]{:S(2)}) collective-permute-start(bf16[256,1024]{1,0:T(8,128)(2,1)S(1)} %add_convert_fusion.9), channel_id=1, source_target_pairs={{1,2},{2,1},{5,6},{6,5},{9,10},{10,9},{13,14},{14,13},{17,18},{18,... | collective-permute-start | bytes 1572872 | tf_op jit(solution)/shard_map/ppermute | solution.py:1205
  362.7 14.9 %collective-permute-start.50 = (bf16[256,1024]{1,0:T(8,128)(2,1)S(1)}, bf16[256,1024]{1,0:T(8,128)(2,1)S(1)}, u32[]{:S(2)}, u32[]{:S(2)}) collective-permute-start(bf16[256,1024]{1,0:T(8,128)(2,1)S(1)} %add_convert_fusion.8), channel_id=1, source_target_pairs={{1,2},{2,1},{5,6},{6,5},{9,10},{10,9},{13,14},{14,13},{17,18},{18,... | collective-permute-start | bytes 1572872 | tf_op jit(solution)/shard_map/ppermute | solution.py:1205
  377.8 21.8 %collective-permute-start.53 = (bf16[256,1024]{1,0:T(8,128)(2,1)S(1)}, bf16[256,1024]{1,0:T(8,128)(2,1)S(1)}, u32[]{:S(2)}, u32[]{:S(2)}) collective-permute-start(bf16[256,1024]{1,0:T(8,128)(2,1)S(1)} %add_convert_fusion.6), channel_id=1, source_target_pairs={{1,0},{2,3},{5,4},{6,7},{9,8},{10,11},{13,12},{14,15},{17,16},{18,... | collective-permute-start | bytes 1572872 | tf_op jit(solution)/shard_map/ppermute | solution.py:1205
  379.2 30.5 %collective-permute-start.54 = (bf16[256,1024]{1,0:T(8,128)(2,1)S(1)}, bf16[256,1024]{1,0:T(8,128)(2,1)S(1)}, u32[]{:S(2)}, u32[]{:S(2)}) collective-permute-start(bf16[256,1024]{1,0:T(8,128)(2,1)S(1)} %add_convert_fusion.7), channel_id=1, source_target_pairs={{1,0},{2,3},{5,4},{6,7},{9,8},{10,11},{13,12},{14,15},{17,16},{18,... | collective-permute-start | bytes 1572872 | tf_op jit(solution)/shard_map/ppermute | solution.py:1205
  382.3 40.1 %collective-permute-start.52 = (bf16[392,1024]{1,0:T(8,128)(2,1)S(1)}, bf16[392,1024]{1,0:T(8,128)(2,1)S(1)}, u32[]{:S(2)}, u32[]{:S(2)}) collective-permute-start(bf16[392,1024]{1,0:T(8,128)(2,1)S(1)} %add_convert_fusion.4), channel_id=1, source_target_pairs={{1,0},{2,3},{5,4},{6,7},{9,8},{10,11},{13,12},{14,15},{17,16},{18,... | collective-permute-start | bytes 2408456 | tf_op jit(solution)/shard_map/ppermute | solution.py:1205
  (125 other events, 1589.6 us)
